TPU v7x, 32 devices: a whole 2x2x4 slice. The times are simulated.
32 devices in a mesh: grp: 2 (over x), row: 8 (over z, y), col: 2 (over core).
Axes of the slice: x: 2, y: 2, z: 4, core: 2. Of those that a mesh axis runs over, the one named last changes fastest.
Arguments:
- upstream: float32 [1024, 384, 256], P(('grp', 'row'), 'col'), parts along dimension 0, may hold values from -6 to 6
- angle_codes: int32 [6, 2], P('grp'), parts along dimension 0, may hold values from 0 to 359
Outputs:
- downstream: float32 [1024, 384, 256], P('grp', 'row', 'col'), parts along dimension 0
There are 2 independent parts, one for each index of `grp`. A program takes and returns all parts, laid end to end along the dimension named above; each array names one. Nothing has to cross between parts.
All inputs are finite; a program needn't handle non-finite values.
Results may differ from a plain program's by a relative error of at most 0.0003.
Values sent between devices are 32-bit elements; how exact they have to be, the bound alone decides.
No kernel may reach another device: no remote copies, remote signals or barrier semaphores. Data moves between devices by JAX's collectives and lax.ppermute only.
A program may use at most 128 MiB of HBM per device.

v0:
```python
import math

import jax
import jax.numpy as jnp
from jax import lax
from jax.sharding import PartitionSpec as P

ANGLES = 360


TWO_PI = 2.0 * math.pi
einsum_forms = ("akl,am->mkl", "kal,am->kml", "kla,am->klm")


def shear_factors_of(angle_codes):
    return jnp.tan((angle_codes.astype(jnp.float32) - ANGLES / 2) * (math.pi / (2 * ANGLES)))


def centred(length, start, total):
    return (lax.iota(jnp.int32, length) + start).astype(jnp.float32) - total / 2


def contract(volume, matrix, along):
    return jnp.einsum(einsum_forms[along], volume, matrix, precision=lax.Precision.HIGHEST)


def shear_back(volume, along, offsets):
    length = volume.shape[along]
    position = lax.iota(jnp.int32, length)
    product = position[:, None] * position[None, :] % length
    angles_grid = product.astype(jnp.float32) * (TWO_PI / length)
    cosines = jnp.cos(angles_grid)
    sines = jnp.sin(angles_grid)
    frequency = jnp.where(position < length // 2, position, position - length).astype(jnp.float32)
    layout = [1, 1, 1]
    layout[along] = length
    phases = frequency.reshape(layout) * offsets * (TWO_PI / length)
    ramp_real = jnp.cos(phases)
    ramp_imag = jnp.sin(phases)
    spectrum_real = contract(volume, cosines, along)
    spectrum_imag = -contract(volume, sines, along)
    turned_real = spectrum_real * ramp_real - spectrum_imag * ramp_imag
    turned_imag = spectrum_real * ramp_imag + spectrum_imag * ramp_real
    return (contract(turned_real, cosines, along) - contract(turned_imag, sines, along)) / length


def body(upstream, angle_codes):
    factors = shear_factors_of(angle_codes)
    row_count = lax.axis_size("row")
    col_count = lax.axis_size("col")
    row_place = lax.axis_index("row")
    col_place = lax.axis_index("col")
    first_local, second_local, third_full = upstream.shape
    first_full = first_local * row_count
    second_full = second_local * col_count
    first_coords = centred(first_local, row_place * first_local, first_full)
    second_coords = centred(second_local, col_place * second_local, second_full)
    offsets = (
        factors[2, 0] * first_coords[:, None, None] + factors[2, 1] * second_coords[None, :, None]
    )
    turned = shear_back(upstream, 2, offsets)
    third_local = third_full // col_count
    second_part = second_full // row_count
    slab_volume = lax.all_to_all(turned, "col", split_axis=0, concat_axis=1, tiled=True)
    slab_width = first_local // col_count
    slab_coords = centred(slab_width, (row_place * col_count + col_place) * slab_width, first_full)
    whole_third = centred(third_full, 0, third_full)
    offsets = (
        factors[1, 0] * slab_coords[:, None, None] + factors[1, 1] * whole_third[None, None, :]
    )
    turned = shear_back(slab_volume, 1, offsets)
    arrived = lax.all_to_all(
        lax.all_to_all(turned, "row", split_axis=1, concat_axis=0, tiled=True),
        "col",
        split_axis=2,
        concat_axis=0,
        tiled=True,
    )
    arrived = arrived.reshape(col_count, row_count, slab_width, second_part, third_local)
    arrived = arrived.transpose(1, 0, 2, 3, 4).reshape(first_full, second_part, third_local)
    out_second = centred(second_part, row_place * second_part, second_full)
    out_third = centred(third_local, col_place * third_local, third_full)
    offsets = factors[0, 0] * out_second[None, :, None] + factors[0, 1] * out_third[None, None, :]
    return shear_back(arrived, 0, offsets)


def solution(mesh):
    placed = (P(("grp", "row"), "col", None), P("grp", None))
    return jax.shard_map(
        body, mesh=mesh, in_specs=placed, out_specs=P("grp", "row", "col"), check_vma=False
    )
```

profile of v0, /device:TPU:0, one launch (start us, length us, event | category | flops | bytes accessed | tf_op | source)
XLA Modules:
  0.0 1031.5 jit_solution(5909526161043933618)
XLA Ops:
  0.0 0.0 copy-start.5
  0.0 17.7 %fusion.119 = f32[256,64,192]{0,2,1:T(8,128)} fusion(f32[64,192,256]{2,1,0:T(8,128)} %param.2), kind=kOutput, calls=%fused_computation.107 | convolution fusion | flops 9664593920 | bytes 25165824 | tf_op jit(solution)/shard_map/kla,am->klm/dot_general | solution.py:24
  17.7 0.0 copy-done.5
  17.7 15.3 %fusion.122 = f32[256,64,192]{0,2,1:T(8,128)} fusion(f32[64,192,256]{2,1,0:T(8,128)S(1)} %copy-done.5), kind=kOutput, calls=%fused_computation.110 | convolution fusion | flops 9664593920 | bytes 25165824 | tf_op jit(solution)/shard_map/kla,am->klm/dot_general | solution.py:24
  33.1 1.0 fusion.225
  34.0 1.0 fusion.233
  35.0 0.0 copy-done.6
  35.1 0.6 fusion.180
  35.7 0.6 add_multiply_fusion.1
  36.3 0.6 add_multiply_fusion.5
  37.0 0.1 broadcast_add_fusion
  37.0 0.0 copy-start.4
  37.0 84.6 %fusion.7 = f32[64,192,256]{2,1,0:T(8,128)S(1)} fusion(f32[256,64,192]{0,2,1:T(8,128)} %fusion.122, f32[256,64,192]{0,2,1:T(8,128)} %fusion.119, f32[64,192]{1,0:T(8,128)S(1)} %broadcast_add_fusion, f32[256]{0:T(256)S(1)} %fusion.135, f32[256,256,1]{1,0,2:T(8,128)S(1)} %fusion.225), kind=kOutput, calls=%fused_computation.11 | convolution fusion | flops 9682550784 | bytes 38061056 | tf_op jit(solution)/shard_map/kla,am->klm/dot_general | solution.py:24
  121.6 0.0 copy-done.3
  121.6 0.0 copy-done.4
  121.6 59.0 %subtract_multiply_fusion.1 = f32[64,192,256]{2,1,0:T(8,128)S(1)} fusion(f32[64,192,256]{2,1,0:T(8,128)S(1)} %fusion.7, f32[256,64,192]{0,2,1:T(8,128)S(1)} %copy-done.4, f32[256,64,192]{0,2,1:T(8,128)S(1)} %copy-done.3, f32[64,192]{1,0:T(8,128)S(1)} %broadcast_add_fusion, f32[256]{0:T(256)S(1)} %fusion.135, f32[256,256,1]{1,0,2:T(8,128)S(1)} %fusion.233), kind=kOutput, calls=%fused_computation.32 | convolution fusion | flops 9688842240 | bytes 50643968 | tf_op jit(solution)/shard_map/kla,am->klm/dot_general | solution.py:24
  180.6 15.9 %all_to_all.51 = f32[64,192,256]{2,1,0:T(8,128)} all-to-all(f32[64,192,256]{2,1,0:T(8,128)S(1)} %subtract_multiply_fusion.1), channel_id=1, replica_groups=mesh['grp'=2,'row'=8,'col'=2] {'col'}, dimensions={0} | all-to-all | bytes 25165824 | tf_op jit(solution)/shard_map/all_to_all | solution.py:64
  196.5 10.8 %copy.24 = f32[32,2,192,256]{3,2,1,0:T(8,128)} copy(f32[32,2,192,256]{3,2,0,1:T(8,128)} %bitcast.163) | data formatting | bytes 25165824 | tf_op jit(solution)/shard_map/all_to_all | solution.py:64
  207.3 33.1 %fusion.83 = f32[384,32,256]{2,0,1:T(8,128)} fusion(f32[32,384,256]{2,1,0:T(8,128)} %bitcast.159), kind=kOutput, calls=%fused_computation.79 | convolution fusion | flops 14496841728 | bytes 25165824 | tf_op jit(solution)/shard_map/kal,am->kml/dot_general | solution.py:24
  240.5 0.0 copy-done
  240.5 31.2 %fusion.86 = f32[384,32,256]{2,0,1:T(8,128)} fusion(f32[32,384,256]{2,1,0:T(8,128)S(1)} %bitcast.160), kind=kOutput, calls=%fused_computation.82 | convolution fusion | flops 14496841728 | bytes 25165824 | tf_op jit(solution)/shard_map/kal,am->kml/dot_general | solution.py:24
  271.7 2.2 fusion.223
  273.9 2.2 fusion.231
  276.1 0.6 add_multiply_fusion
  276.8 0.6 add_multiply_fusion.4
  277.3 0.1 broadcast_add_fusion.1
  277.4 70.5 %fusion.1 = f32[384,32,256]{2,0,1:T(8,128)S(1)} fusion(f32[384,32,256]{2,0,1:T(8,128)} %fusion.86, f32[384,32,256]{2,0,1:T(8,128)} %fusion.83, f32[32,256]{1,0:T(8,128)S(1)} %broadcast_add_fusion.1, f32[384]{0:T(512)S(1)} %fusion.133, f32[384,384,1]{0,1,2:T(8,128)S(1)} %fusion.223), kind=kOutput, calls=%fused_computation.3 | convolution fusion | flops 14514388992 | bytes 38372864 | tf_op jit(solution)/shard_map/kal,am->kml/dot_general | solution.py:24
  347.9 72.5 %multiply_bitcast_fusion = f32[32,384,256]{2,1,0:T(8,128)} fusion(f32[384,32,256]{2,0,1:T(8,128)S(1)} %fusion.1, f32[384,32,256]{2,0,1:T(8,128)} %fusion.86, f32[384,32,256]{2,0,1:T(8,128)} %fusion.83, f32[32,256]{1,0:T(8,128)S(1)} %broadcast_add_fusion.1, f32[384]{0:T(512)S(1)} %fusion.133, f32[384,384,1]{0,1,2:T(8,128)S(1)} %fusion.231), kind=kOutput, calls=%fused_computation.28 | convolution fusion | flops 14520680448 | bytes 50955776 | tf_op jit(solution)/shard_map/kal,am->kml/dot_general | solution.py:24
  420.4 16.6 %copy.25 = f32[32,384,256]{2,0,1:T(8,128)} copy(f32[32,384,256]{2,1,0:T(8,128)} %multiply_bitcast_fusion) | data formatting | bytes 25165824 | tf_op jit(solution)/shard_map/div | solution.py:44
  437.0 7.5 all-to-all-start.1
  444.5 0.6 add_multiply_fusion.3
  445.1 0.7 add_multiply_fusion.2
  445.8 3.8 fusion.229
  449.6 3.8 fusion.227
  453.4 0.1 broadcast_add_fusion.2
  453.5 264.1 %all-to-all-done.1 = f32[32,384,256]{2,0,1:T(8,128)} async-done(((f32[32,384,256]{2,0,1:T(8,128)}), f32[32,384,256]{2,0,1:T(8,128)}, u32[]{:S(2)}, u32[]{:S(2)}) %all-to-all-start.1) | async-done | bytes 12582944 | tf_op jit(solution)/shard_map/all_to_all | solution.py:73
  717.6 16.9 %copy.27 = f32[8,32,48,256]{3,2,1,0:T(8,128)} copy(f32[8,32,48,256]{3,1,2,0:T(8,128)} %bitcast.19) | data formatting | bytes 25165824 | tf_op jit(solution)/shard_map/all_to_all | solution.py:73
  734.6 12.9 %copy.28 = f32[256,48,256]{0,1,2:T(8,128)} copy(f32[256,48,256]{2,1,0:T(8,128)} %bitcast.164) | data formatting | bytes 25165824 | tf_op jit(solution)/shard_map/all_to_all | solution.py:73
  747.5 25.0 %all_to_all.52 = f32[256,48,256]{0,1,2:T(8,128)} all-to-all(f32[256,48,256]{0,1,2:T(8,128)} %copy.28), channel_id=1, replica_groups=mesh['grp'=2,'row'=8,'col'=2] {'col'}, dimensions={2} | all-to-all | bytes 25165824 | tf_op jit(solution)/shard_map/all_to_all | solution.py:72
  772.5 12.8 %copy.30 = f32[2,256,48,128]{3,2,1,0:T(8,128)} copy(f32[2,256,48,128]{1,2,3,0:T(8,128)} %bitcast.165) | data formatting | bytes 25165824 | tf_op jit(solution)/shard_map/all_to_all | solution.py:72
  785.3 13.1 %copy.31 = f32[8,2,32,48,128]{4,2,1,0,3:T(8,128)} copy(f32[8,2,32,48,128]{4,3,2,0,1:T(8,128)} %bitcast.166) | data formatting | bytes 25165824 | tf_op jit(solution)/shard_map/transpose | solution.py:80
  798.4 36.3 %fusion.72 = f32[512,48,128]{2,0,1:T(8,128)S(1)} fusion(f32[512,48,128]{2,0,1:T(8,128)} %bitcast.161), kind=kOutput, calls=%fused_computation.67 | convolution fusion | flops 19331022848 | bytes 25165824 | tf_op jit(solution)/shard_map/akl,am->mkl/dot_general | solution.py:24
  834.7 0.0 copy-done.1
  834.7 34.2 %fusion.75 = f32[512,48,128]{2,0,1:T(8,128)} fusion(f32[512,48,128]{2,0,1:T(8,128)S(1)} %bitcast.162), kind=kOutput, calls=%fused_computation.70 | convolution fusion | flops 19331022848 | bytes 25165824 | tf_op jit(solution)/shard_map/akl,am->mkl/dot_general | solution.py:24
  868.9 72.9 %fusion.12 = f32[512,48,128]{2,0,1:T(8,128)} fusion(f32[512,48,128]{2,0,1:T(8,128)} %fusion.75, f32[512,48,128]{2,0,1:T(8,128)S(1)} %fusion.72, f32[48,128]{1,0:T(8,128)S(1)} %broadcast_add_fusion.2, f32[512]{0:T(512)S(1)} %fusion.134, f32[512,512,1]{0,1,2:T(8,128)S(1)} %fusion.229), kind=kOutput, calls=%fused_computation.17 | convolution fusion | flops 19346227200 | bytes 38823936 | tf_op jit(solution)/shard_map/akl,am->mkl/dot_general | solution.py:24
  941.8 0.0 copy-done.2
  941.8 72.8 %subtract_multiply_fusion = f32[512,48,128]{2,0,1:T(8,128)} fusion(f32[512,48,128]{2,0,1:T(8,128)} %fusion.12, f32[512,48,128]{2,0,1:T(8,128)S(1)} %copy-done.2, f32[512,48,128]{2,0,1:T(8,128)S(1)} %fusion.72, f32[48,128]{1,0:T(8,128)S(1)} %broadcast_add_fusion.2, f32[512]{0:T(512)S(1)} %fusion.134, f32[512,512,1]{0,1,2:T(8,128)S(1)} %fusion.227), kind=kOutput, calls=%fused_computation.16 | convolution fusion | flops 19352518656 | bytes 51406848 | tf_op jit(solution)/shard_map/akl,am->mkl/dot_general | solution.py:24
  1014.6 16.6 %copy.32 = f32[512,48,128]{2,1,0:T(8,128)} copy(f32[512,48,128]{2,0,1:T(8,128)} %subtract_multiply_fusion) | data formatting | bytes 25165824 | tf_op jit(solution)/shard_map/div | solution.py:44
  (9 shorter events, 0.1 us)
Async XLA Ops:
  0.0 17.7 %copy-start.5 = (f32[64,192,256]{2,1,0:T(8,128)S(1)}, f32[64,192,256]{2,1,0:T(8,128)}, u32[]{:S(2)}) copy-start(f32[64,192,256]{2,1,0:T(8,128)} %param.2) | copy-start | bytes 37748740
  17.7 17.3 %copy-start.6 = (s32[3,2]{0,1:T(2,128)S(1)}, s32[3,2]{0,1:T(2,128)}, u32[]{:S(2)}) copy-start(s32[3,2]{0,1:T(2,128)} %param.3) | copy-start | bytes 76
  37.0 84.6 %copy-start.3 = (f32[256,64,192]{0,2,1:T(8,128)S(1)}, f32[256,64,192]{0,2,1:T(8,128)}, u32[]{:S(2)}) copy-start(f32[256,64,192]{0,2,1:T(8,128)} %fusion.119) | copy-start | bytes 37748740
  37.0 84.6 %copy-start.4 = (f32[256,64,192]{0,2,1:T(8,128)S(1)}, f32[256,64,192]{0,2,1:T(8,128)}, u32[]{:S(2)}) copy-start(f32[256,64,192]{0,2,1:T(8,128)} %fusion.122) | copy-start | bytes 37748740
  207.3 33.1 %copy-start = (f32[32,2,192,256]{3,2,1,0:T(8,128)S(1)}, f32[32,2,192,256]{3,2,1,0:T(8,128)}, u32[]{:S(2)}) copy-start(f32[32,2,192,256]{3,2,1,0:T(8,128)} %copy.24) | copy-start | bytes 37748740
  437.0 280.6 %all-to-all-start.1 = ((f32[32,384,256]{2,0,1:T(8,128)}), f32[32,384,256]{2,0,1:T(8,128)}, u32[]{:S(2)}, u32[]{:S(2)}) async-start(f32[32,384,256]{2,0,1:T(8,128)} %copy.25), calls=%async_computation.1 | async-start | bytes 25165824 | tf_op jit(solution)/shard_map/all_to_all | solution.py:73
  798.4 36.3 %copy-start.1 = (f32[8,2,32,48,128]{4,2,1,0,3:T(8,128)S(1)}, f32[8,2,32,48,128]{4,2,1,0,3:T(8,128)}, u32[]{:S(2)}) copy-start(f32[8,2,32,48,128]{4,2,1,0,3:T(8,128)} %copy.31) | copy-start | bytes 37748740
  868.9 72.9 %copy-start.2 = (f32[512,48,128]{2,0,1:T(8,128)S(1)}, f32[512,48,128]{2,0,1:T(8,128)}, u32[]{:S(2)}) copy-start(f32[512,48,128]{2,0,1:T(8,128)} %fusion.75) | copy-start | bytes 37748740
where the time goes:
time: 1040 us; the launch traced here: 1030 us
  matrix products  600 us (58%)
  waiting for transfers between devices  264 us (25%)
  local copies, waits for them, and re-layouts  101 us (10%)
  blocking collectives  40.9 us (4%)
  other arithmetic  18 us (2%)
    dot_general x12, matrix products, contract(): jnp.einsum(einsum_forms[along], volume, matrix, precision=lax.Precision.H...  600 us
    all_to_all x1, waiting for transfers between devices, body(): lax.all_to_all(turned, 'row', split_axis=1, concat_axis=0, tiled=True)  264 us
    div x2, local copies, waits for them, and re-layouts, shear_back(): (contract(turned_real, cosines, along) - contract(turned_imag, sines, alo...  33.3 us
    all_to_all x2, local copies, waits for them, and re-layouts, body(): lax.all_to_all(turned, 'row', split_axis=1, concat_axis=0, tiled=True)  29.8 us
    all_to_all x1, blocking collectives, body(): lax.all_to_all(lax.all_to_all(turned, 'row', split_axis=1, concat_axis=0,...  25 us
  transfers between devices with their start and end apart: 1, of which 1 were waited for; matrix products, arithmetic and copies ran while one was open for 1% of the time, Pallas kernels for 0%

commit v1 on v0

v1 whole, which is shorter than its diff:
```python
import functools
import math

import jax
import jax.numpy as jnp
import ml_dtypes
import numpy as np
from jax import lax
from jax.experimental import pallas as pl
from jax.experimental.pallas import tpu as pltpu
from jax.sharding import PartitionSpec as P

ANGLES = 360
F32 = jnp.float32
BF16 = jnp.bfloat16
VMEM_LIMIT = 58 * 1024 * 1024
XB = 4
HEAD = 2
CHUNKS = (3, 2, 1)
WINDOW = 5


def shear_factors_of(angle_codes):
    return jnp.tan((angle_codes.astype(F32) - ANGLES / 2) * (math.pi / (2 * ANGLES)))


def halves(matrix):
    high = matrix.astype(ml_dtypes.bfloat16)
    low = (matrix - high.astype(np.float64)).astype(ml_dtypes.bfloat16)
    return high, low


def direct_matrices(n):
    m = np.arange(n)
    f = np.arange(n // 2)
    theta = 2 * np.pi * ((m[:, None] * f[None, :]) % n) / n
    cosines, sines = np.cos(theta), np.sin(theta)
    sines[:, 0] = (-1.0) ** m
    weight = np.full(n // 2, 2.0 / n)
    weight[0] = 1.0 / n
    forward = np.concatenate([cosines, sines], 1)
    inverse = np.concatenate([cosines * weight, sines * weight], 1).T
    return forward, inverse


def split_matrices(n):
    half = n // 2
    m = np.arange(half)
    j = np.arange(half // 2)
    out = []
    for odd in (0, 1):
        theta = 2 * np.pi * (((2 * j + odd)[:, None] * m[None, :]) % n) / n
        cosines, sines = np.cos(theta), np.sin(theta)
        weight = np.full((half // 2, 1), 2.0 / n)
        if not odd:
            sines[0] = (-1.0) ** m
            weight[0] = 1.0 / n
        out.append(np.concatenate([cosines, sines], 0))
        out.append(np.concatenate([cosines * weight, sines * weight], 0).T)
    return out


def frequencies_split(n):
    j = np.arange(n // 4)
    even = 2 * j
    even[0] = n // 2
    return np.concatenate([even, 2 * j + 1]).astype(np.float32)


def lhs3(matrix):
    high, low = halves(matrix)
    return jnp.asarray(np.concatenate([high, high, low], 1))


def rhs3(matrix):
    high, low = halves(matrix)
    return jnp.asarray(np.concatenate([high, high, low], 0))


def split(value):
    high = value.astype(BF16)
    low = (value - high.astype(F32)).astype(BF16)
    return high, low


def turn(c, s, c1, s1, c2, s2, first):
    cp = c1 * c2 - s1 * s2
    sp = s1 * c2 + c1 * s2
    cpc = cp
    if first is not None:
        cpc = jnp.where(first, 1.0, cp)
        sp = jnp.where(first, 0.0, sp)
    return c * cpc + s * sp, s * cp - c * sp


def dot(a, b):
    return jnp.dot(a, b, preferred_element_type=F32)


def turns(frequency, offsets, n):
    u = frequency * offsets * (1.0 / n)
    p = (u - jnp.round(u)) * (2.0 * math.pi)
    return jnp.cos(p), jnp.sin(p)


def iota(shape, dim):
    return lax.broadcasted_iota(jnp.int32, shape, dim)


def third_kernel(x0, size, full, place, slopes, v_ref, fw_ref, iv_ref, own_ref, other_ref, c1_scr, s1_scr, c2_scr, s2_scr):
    xb, ny, n = v_ref.shape
    half = n // 2
    step = pl.program_id(0)

    @pl.when(step == 0)
    def _():
        def offsets(count, start, total, slope):
            return slope * ((iota((count, half), 0) + start).astype(F32) - total / 2)

        def frequency(count):
            f = iota((count, half), 1)
            return jnp.where(f == 0, half, f).astype(F32)

        padded = c1_scr.shape[0]
        c1_scr[...], s1_scr[...] = turns(
            frequency(padded), offsets(padded, place[1] + x0, full[0], slopes[4]), n
        )
        c2_scr[...], s2_scr[...] = turns(frequency(ny), offsets(ny, place[2] * ny, full[1], slopes[5]), n)

    v = v_ref[...].reshape(xb * ny, n)
    high, low = split(v)
    spectrum = dot(jnp.concatenate([high, low, high], 1), fw_ref[...])
    first = iota((ny, half), 1) == 0
    parts = []
    for x in range(xb):
        rows = slice(x * ny, (x + 1) * ny)
        at = pl.ds(step * xb + x, 1)
        c, s = turn(
            spectrum[rows, :half], spectrum[rows, half:],
            c1_scr[at, :], s1_scr[at, :], c2_scr[...], s2_scr[...], first,
        )
        parts.append(jnp.concatenate([c, s], 1))
    high, low = split(jnp.concatenate(parts, 0))
    back = dot(jnp.concatenate([high, low, high], 1), iv_ref[...])
    lower = back[:, :half].reshape(xb, ny, half)
    upper = back[:, half:].reshape(xb, ny, half)
    mine = place[2] == 0
    own_ref[...] = jnp.where(mine, lower, upper)
    other_ref[...] = jnp.where(mine, upper, lower)


def second_kernel(
    x0, heights, part, full, place, slopes, own_ref, other_ref, fe_ref, fo_ref, ie_ref, io_ref, *rest
):
    if heights:
        outs, (c1_scr, s1_scr, c2_scr, s2_scr, p_scr, q_scr) = rest[:-6], rest[-6:]
    else:
        (out,), (c1_scr, s1_scr, c2_scr, s2_scr) = rest[:-4], rest[-4:]
    xb, half, nk = own_ref.shape
    n = 2 * half
    quarter = half // 2
    blocks = half // part
    step = pl.program_id(0)

    @pl.when(step == 0)
    def _():
        def frequency(width):
            r = iota((half, width), 0)
            f = jnp.where(r < quarter, 2 * r, 2 * (r - quarter) + 1)
            return jnp.where(r == 0, half, f).astype(F32)

        lanes = iota((half, 128), 1)
        c1, s1 = turns(frequency(128), slopes[2] * ((lanes + (place[1] + x0)).astype(F32) - full[0] / 2), n)
        for b in range(c1_scr.shape[0]):
            c1_scr[b] = c1[:, b * xb : (b + 1) * xb]
            s1_scr[b] = s1[:, b * xb : (b + 1) * xb]
        lanes = iota((half, nk), 1)
        c2_scr[...], s2_scr[...] = turns(
            frequency(nk), slopes[3] * ((lanes + place[2] * nk).astype(F32) - full[2] / 2), n
        )

    col_sign = (1 - 2 * place[2]).astype(F32)
    row_sign = (1 - 2 * place[3]).astype(F32)
    first = iota((quarter, nk), 0) == 0
    for x0 in range(0, xb, 2):
        pair = (x0, x0 + 1)
        total = jnp.concatenate([own_ref[x] + other_ref[x] for x in pair], 1)
        delta = jnp.concatenate([own_ref[x] - other_ref[x] for x in pair], 1) * col_sign
        results = []
        for odd, (value, fw, iv) in enumerate(((total, fe_ref, ie_ref), (delta, fo_ref, io_ref))):
            high, low = split(value)
            spectrum = dot(fw[...], jnp.concatenate([high, low, high], 0))
            frows = slice(odd * quarter, (odd + 1) * quarter)
            c2, s2 = c2_scr[frows], s2_scr[frows]
            turned = []
            for k, x in enumerate(pair):
                lanes = slice(k * nk, (k + 1) * nk)
                c, s = turn(
                    spectrum[:quarter, lanes], spectrum[quarter:, lanes],
                    c1_scr[step, frows, x : x + 1], s1_scr[step, frows, x : x + 1], c2, s2,
                    None if odd else first,
                )
                turned.append(jnp.concatenate([c, s], 0))
            high, low = split(jnp.concatenate(turned, 1))
            results.append(dot(iv[...], jnp.concatenate([high, low, high], 0)))
        p, q = results
        if not heights:
            for base, value in ((0, p + q), (blocks, p - q)):
                for j in range(blocks):
                    for k, x in enumerate(pair):
                        out[base + j, x] = value[j * part : (j + 1) * part, k * nk : (k + 1) * nk]
            continue
        q = q * row_sign
        for j in range(blocks):
            p_scr[j] = p[j * part : (j + 1) * part]
            q_scr[j] = q[j * part : (j + 1) * part]
        for j in range(blocks):
            source = lax.bitwise_xor(place[0], j)
            p, q = p_scr[source], q_scr[source]
            for slot, value in ((j, p + q), (j + blocks, p - q)):
                y = 0
                for c, height in enumerate(heights):
                    for k, x in enumerate(pair):
                        outs[slot * len(heights) + c][x] = value[y : y + height, k * nk : (k + 1) * nk]
                    y += height


def first_kernel(place, slopes, head_ref, *refs):
    slots = head_ref.shape[0]
    blocks = slots // 2
    ins, rest = refs[:slots], refs[slots:]
    fe_ref, fo_ref, ie_ref, io_ref, c1_ref, s1_ref, c2_ref, s2_ref = rest[:8]
    out_ref, token_ref, e_scr, o_scr = rest[-4:]
    token_ref[...] = jnp.zeros_like(token_ref)
    n, ny, nk = out_ref.shape
    half, quarter = n // 2, n // 4
    heads, tails = head_ref.shape[1], ins[0].shape[0]
    row_sign = (1 - 2 * place[3]).astype(F32)
    first = iota((quarter, nk), 0) == 0
    aligned = ny % 8 == 0

    def flatten(ref):
        return ref.reshape(math.prod(ref.shape[:-1]), nk) if aligned else ref

    flat_head, flat, out_flat = flatten(head_ref), [flatten(ref) for ref in ins], flatten(out_ref)

    def head(side, y):
        if aligned:
            return flat_head[pl.ds(side * blocks * heads * ny + y, blocks * heads, stride=ny), :]
        return head_ref[side * blocks : (side + 1) * blocks, :, y, :].reshape(blocks * heads, nk)

    def column(slot, y):
        if aligned:
            return flat[slot][pl.ds(y, tails, stride=ny), :]
        return ins[slot][:, y, :]

    def keep(scr, at, count, value):
        high, low = split(value)
        for k, part in enumerate((high, low, high)):
            start = at + k * half
            if not isinstance(start, int):
                start = pl.multiple_of(start, 8)
            scr[pl.ds(start, count), :] = part

    for y0 in range(0, ny, 2):
        pair = (y0, y0 + 1)
        near = jnp.concatenate([head(0, y) for y in pair], 1)
        far = jnp.concatenate([head(1, y) for y in pair], 1)
        keep(e_scr, 0, blocks * heads, near + far)
        keep(o_scr, 0, blocks * heads, near - far)
        for j in range(blocks):
            at = lax.bitwise_xor(place[0], j) * tails + blocks * heads
            near = jnp.concatenate([column(j, y) for y in pair], 1)
            far = jnp.concatenate([column(j + blocks, y) for y in pair], 1)
            keep(e_scr, at, tails, near + far)
            keep(o_scr, at, tails, (near - far) * row_sign)
        results = []
        for odd, (scr, fw, iv) in enumerate(((e_scr, fe_ref, ie_ref), (o_scr, fo_ref, io_ref))):
            spectrum = dot(fw[...], scr[...])
            frows = slice(odd * quarter, (odd + 1) * quarter)
            c2, s2 = c2_ref[frows], s2_ref[frows]
            turned = []
            for k, y in enumerate(pair):
                lanes = slice(k * nk, (k + 1) * nk)
                c, s = turn(
                    spectrum[:quarter, lanes], spectrum[quarter:, lanes],
                    c1_ref[0, frows, y : y + 1], s1_ref[0, frows, y : y + 1], c2, s2,
                    None if odd else first,
                )
                turned.append(jnp.concatenate([c, s], 0))
            high, low = split(jnp.concatenate(turned, 1))
            results.append(dot(iv[...], jnp.concatenate([high, low, high], 0)))
        p, q = results
        for at, value in ((0, p + q), (half, p - q)):
            for k, y in enumerate(pair):
                column_out = value[:, k * nk : (k + 1) * nk]
                if aligned:
                    out_flat[pl.ds(at * ny + y, half, stride=ny), :] = column_out
                else:
                    out_ref[at : at + half, y, :] = column_out


def whole(array):
    rank = array.ndim
    return pl.BlockSpec(array.shape, lambda i, *_: (0,) * rank)


def call(kernel, grid, in_specs, out_specs, out_shape, scratch, flops, moved, aliases=None, name=None):
    return pl.pallas_call(
        kernel,
        out_shape=out_shape,
        grid_spec=pltpu.PrefetchScalarGridSpec(
            num_scalar_prefetch=2, grid=(grid,), in_specs=in_specs, out_specs=out_specs, scratch_shapes=scratch
        ),
        input_output_aliases=aliases or {},
        compiler_params=pltpu.CompilerParams(vmem_limit_bytes=VMEM_LIMIT),
        cost_estimate=pl.CostEstimate(flops=1, bytes_accessed=1, transcendentals=0),
        name=name,
    )


def body(upstream, angle_codes):
    factors = shear_factors_of(angle_codes)
    row_count, col_count = lax.axis_size("row"), lax.axis_size("col")
    row_place, col_place = lax.axis_index("row"), lax.axis_index("col")
    xl, yl, nz = upstream.shape
    nx, ny = xl * row_count, yl * col_count
    full = (nx, ny, nz)
    nk, part = nz // col_count, ny // row_count
    blocks = row_count // 2
    xb = XB
    head_x = xl * HEAD // 8 if xl >= 64 else xl // 2
    tail_x = xl - head_x
    heights = tuple(part * sixths // 6 for sixths in CHUNKS) if part % 48 == 0 else (part,)
    rows = 8 if part % 8 == 0 else part
    place = jnp.stack([row_place % blocks, row_place * xl, col_place, row_place // blocks]).astype(jnp.int32)
    slopes = factors.reshape(-1)

    z_forward, z_inverse = (rhs3(matrix) for matrix in direct_matrices(nz))
    y_mats = [lhs3(matrix) for matrix in split_matrices(ny)]
    y_mats = [y_mats[0], y_mats[2], y_mats[1], y_mats[3]]
    places = np.arange(nx // 2).reshape(blocks, xl)
    arrival = np.concatenate([places[:, :head_x].reshape(-1), places[:, head_x:].reshape(-1)])
    x_even, x_even_back, x_odd, x_odd_back = split_matrices(nx)
    x_mats = [lhs3(matrix) for matrix in (x_even[:, arrival], x_odd[:, arrival], x_even_back, x_odd_back)]

    def third(x0, size, volume):
        base = x0 // xb
        out = pl.BlockSpec((xb, yl, nk), lambda i, *_: (i, 0, 0))
        near = pltpu.VMEM((-(-size // 8) * 8, nz // 2), F32)
        far = pltpu.VMEM((yl, nz // 2), F32)
        return call(
            functools.partial(third_kernel, x0, size, full), size // xb,
            [pl.BlockSpec((xb, yl, nz), lambda i, *_: (base + i, 0, 0)), whole(z_forward), whole(z_inverse)],
            [out, out],
            [jax.ShapeDtypeStruct((size, yl, nk), F32)] * 2,
            [near, near, far, far], 12 * size * yl * nz * nz, 8 * size * yl * nz, name="third",
        )(place, slopes, volume, z_forward, z_inverse)

    def second(x0, size, own, other, heights):
        data = pl.BlockSpec((xb, yl, nk), lambda i, *_: (i, 0, 0))
        near = pltpu.VMEM((size // xb, ny // 2, xb), F32)
        far = pltpu.VMEM((ny // 2, nk), F32)
        scratch = [near, near, far, far]
        if heights:
            scratch += [pltpu.VMEM((blocks, part, 2 * nk), F32)] * 2
            specs = [pl.BlockSpec((xb, height, nk), lambda i, *_: (i, 0, 0)) for height in heights] * row_count
            shapes = [jax.ShapeDtypeStruct((size, height, nk), F32) for height in heights] * row_count
        else:
            specs = [pl.BlockSpec((row_count, xb, part, nk), lambda i, *_: (0, i, 0, 0))]
            shapes = [jax.ShapeDtypeStruct((row_count, size, part, nk), F32)]
        return call(
            functools.partial(second_kernel, x0, heights, part, full), size // xb,
            [data, data] + [whole(matrix) for matrix in y_mats],
            specs, shapes, scratch, 6 * size * ny * nk * ny, 8 * size * ny * nk, name="second",
        )(place, slopes, own, other, *y_mats)

    sent = []
    order = [d for pair in zip(range(blocks, row_count), range(blocks)) for d in pair if d]

    def after(value, *others):
        return lax.optimization_barrier((value, *others))[0]

    def spread(pieces, gates=None):
        got = [pieces[0]] + [None] * (row_count - 1)
        for i, d in enumerate(order):
            others = list(sent[-WINDOW:][:1]) if len(sent) >= WINDOW else []
            if gates and i in gates:
                others.append(gates[i])
            got[d] = lax.ppermute(after(pieces[d], *others), "row", [(i, i ^ d) for i in range(row_count)])
            sent.append(got[d])
        return got

    swap = [(0, 1), (1, 0)]
    own, other = third(0, head_x, upstream)
    (head,) = second(0, head_x, own, lax.ppermute(other, "col", swap), None)
    volume = after(upstream, head)
    head = lax.all_to_all(head, "row", 0, 0, tiled=True)
    own, other = third(head_x, tail_x, volume)
    outs = second(head_x, tail_x, own, lax.ppermute(other, "col", swap), heights)
    pieces = [[outs[d * len(heights) + c] for d in range(row_count)] for c in range(len(heights))]

    def waves(frequency, offsets, n):
        p = frequency * offsets * (2.0 * math.pi / n)
        return jnp.cos(p), jnp.sin(p)

    def centred(length, start, total):
        return (lax.iota(jnp.int32, length) + start).astype(F32) - total / 2

    late = after(slopes, outs[0])
    fx = frequencies_split(nx)
    xc1, xs1 = waves(fx[None, :, None], (late[0] * centred(part, row_place * part, ny)).reshape(-1, 1, rows), nx)
    xc2, xs2 = waves(fx[:, None], (late[1] * centred(nk, col_place * nk, nz))[None, :], nx)

    def first(y0, height, got, result, token):
        base = y0 // rows
        ins = [head, *got]
        specs = [pl.BlockSpec((row_count, head_x, rows, nk), lambda i, *_: (0, 0, base + i, 0))]
        specs += [pl.BlockSpec((tail_x, rows, nk), lambda i, *_: (0, i, 0))] * row_count
        table = pl.BlockSpec((1, nx // 2, rows), lambda i, *_: (base + i, 0, 0))
        ins += [*x_mats, xc1, xs1, xc2, xs2]
        specs += [whole(matrix) for matrix in x_mats] + [table, table, whole(xc2), whole(xs2)]
        aliases = {}
        if result is not None:
            aliases = {len(ins) + 2: 0}
            ins += [result, token]
            specs += [pl.BlockSpec(memory_space=pl.ANY)] * 2
        scratch = pltpu.VMEM((3 * nx // 2, 2 * nk), BF16)
        return call(
            first_kernel, height // rows,
            specs,
            [pl.BlockSpec((nx, rows, nk), lambda i, *_: (0, base + i, 0)), pl.BlockSpec((8, 128), lambda i, *_: (0, 0))],
            [jax.ShapeDtypeStruct((nx, part, nk), F32), jax.ShapeDtypeStruct((8, 128), F32)],
            [scratch, scratch], 6 * nx * height * nk * nx, 8 * nx * height * nk, aliases, name="first",
        )(place, slopes, *ins)

    result, token, tokens, y0 = None, None, [], 0
    got = [spread(pieces[0], {i: head for i in range(WINDOW)})]
    for c, height in enumerate(heights):
        ahead = c + 1
        if ahead < len(heights):
            gates = {}
            if c >= 1:
                gates[0] = tokens[c - 1]
            if ahead == len(heights) - 1 and c >= 1:
                result, token = first(y0, height, got[c], result, token)
                tokens.append(token)
                gates[len(order) - 2] = token
            got.append(spread(pieces[ahead], gates))
        if len(tokens) == c:
            result, token = first(y0, height, got[c], result, token)
            tokens.append(token)
        y0 += height
    return result


def solution(mesh):
    placed = (P(("grp", "row"), "col", None), P("grp", None))
    return jax.shard_map(
        body, mesh=mesh, in_specs=placed, out_specs=P("grp", "row", "col"), check_vma=False
    )
```

time: 1040 us -> 321 us (0.31)
  matrix products: 600 us -> 0 us
  local copies, waits for them, and re-layouts: 101 us -> 3.21 us
  waiting for transfers between devices: 264 us -> 175 us
  Pallas kernels: 0 us -> 87.8 us
  blocking collectives: 40.9 us -> 0 us
  starting transfers between devices: 7.46 us -> 45.2 us
    dot_general x12 -> x0, matrix products: 600 us -> none  [contract(): jnp.einsum(einsum_forms[along], volume, matrix, precision=lax.Precision.H...]
    all_to_all x1, waiting for transfers between devices: 264 us -> 23.3 us  [body(): head = lax.all_to_all(head, 'row', 0, 0, tiled=True)]
    ppermute x0 -> x23, waiting for transfers between devices: none -> 152 us  [the longest x21 141 us: spread(): lax.ppermute(after(pieces[d], *others), 'row', [(i, i ^ d) for i in range...]
    pallas_call x0 -> x7, Pallas kernels: none -> 87.8 us  [the longest x3 30.8 us: first(): call(first_kernel, height // rows, specs, [pl.BlockSpec((nx, rows, nk), l...]
    all_to_all x4 -> x0, local copies, waits for them, and re-layouts: 53.4 us -> none  [the longest x2 29.8 us: body(): lax.all_to_all(turned, 'row', split_axis=1, concat_axis=0, tiled=True)]
    all_to_all x2 -> x0, blocking collectives: 40.9 us -> none  [the longest x1 25 us: body(): lax.all_to_all(lax.all_to_all(turned, 'row', split_axis=1, concat_axis=0,...]
    ppermute x0 -> x23, starting transfers between devices: none -> 38 us  [the longest x21 37.5 us: spread(): lax.ppermute(after(pieces[d], *others), 'row', [(i, i ^ d) for i in range...]
    div x2 -> x0, local copies, waits for them, and re-layouts: 33.3 us -> none  [shear_back(): (contract(turned_real, cosines, along) - contract(turned_imag, sines, alo...]
  transfers between devices with their start and end apart: 1 -> 24, of which waited for: 1 -> 11; matrix products, arithmetic and copies ran while one was open for 1% -> 2% of each run, Pallas kernels for 0% -> 20%
where the time goes in v1:
time: 321 us; the launch traced here: 319 us
  waiting for transfers between devices  175 us (55%)
  Pallas kernels  87.8 us (27%)
  starting transfers between devices  45.2 us (14%)
  other arithmetic  7.68 us (2%)
  local copies, waits for them, and re-layouts  3.21 us (1%)
    ppermute x21, waiting for transfers between devices, spread(): lax.ppermute(after(pieces[d], *others), 'row', [(i, i ^ d) for i in range...  141 us
    ppermute x21, starting transfers between devices, spread(): lax.ppermute(after(pieces[d], *others), 'row', [(i, i ^ d) for i in range...  37.5 us
    pallas_call x3, Pallas kernels, first(): call(first_kernel, height // rows, specs, [pl.BlockSpec((nx, rows, nk), l...  30.8 us
    pallas_call x2, Pallas kernels, second(): call(functools.partial(second_kernel, x0, heights, part, full), size // x...  28.6 us
    pallas_call x2, Pallas kernels, third(): call(functools.partial(third_kernel, x0, size, full), size // xb, [pl.Blo...  28.5 us
    all_to_all x1, waiting for transfers between devices, body(): head = lax.all_to_all(head, 'row', 0, 0, tiled=True)  23.3 us
    ppermute x1, waiting for transfers between devices, body(): lax.ppermute(other, 'col', swap)  8.25 us
    all_to_all x1, starting transfers between devices, body(): head = lax.all_to_all(head, 'row', 0, 0, tiled=True)  7.2 us
  transfers between devices with their start and end apart: 24, of which 11 were waited for; matrix products, arithmetic and copies ran while one was open for 2% of the time, Pallas kernels for 20%

profile of v1, /device:TPU:0, one launch (start us, length us, event | category | flops | bytes accessed | tf_op | source)
XLA Modules:
  0.0 319.4 jit_solution(6770118994038754361)
XLA Ops:
  0.0 0.7 multiply_tan_fusion
  0.7 0.1 copy.18
  0.8 0.7 reshape.22.slopes
  1.5 0.6 pad_add_fusion.place
  2.0 8.7 %third.2 = (f32[16,192,128]{2,1,0:T(8,128)}, f32[16,192,128]{2,1,0:T(8,128)}) custom-call(s32[4]{0:T(128)} %pad_add_fusion.place, f32[6]{0:T(128)} %reshape.22.slopes, f32[64,192,256]{2,1,0:T(8,128)} %v_ref.2, bf16[768,256]{1,0:T(8,128)(2,1)} %constant.82.clone.fw_ref, bf16[768,256]{1,0:T(8,128)(2,1)} %constant.83.clone.iv_ref), custom_call_target="tpu_custom_call" | custom-call | flops 1 | bytes 1 | tf_op jit(solution)/shard_map/third/pallas_call | solution.py:352
  10.8 0.5 collective-permute-start
  11.2 3.2 %collective-permute-done.other_ref = f32[16,192,128]{2,1,0:T(8,128)S(1)} collective-permute-done((f32[16,192,128]{2,1,0:T(8,128)}, f32[16,192,128]{2,1,0:T(8,128)S(1)}, u32[]{:S(2)}, u32[]{:S(2)}) %collective-permute-start) | collective-permute-done | bytes 1572896 | tf_op jit(solution)/shard_map/ppermute | solution.py:396
  14.5 1.2 copy-done.1
  15.6 8.8 %second.2 = f32[8,16,48,128]{3,2,1,0:T(8,128)} custom-call(s32[4]{0:T(128)} %pad_add_fusion.place, f32[6]{0:T(128)} %reshape.22.slopes, f32[16,192,128]{2,1,0:T(8,128)} %get-tuple-element.61.own_ref, f32[16,192,128]{2,1,0:T(8,128)} %copy-done.1, bf16[192,576]{1,0:T(8,128)(2,1)} %constant.84.clone.fe_ref, bf16[192,576]{1,0:T(8,128)(2,1)} %constant.86.clone.fo_ref, ...), custom_call_target="tpu_custom_call" | custom-call | flops 1 | bytes 1 | tf_op jit(solution)/shard_map/second/pallas_call | solution.py:372
  24.5 7.2 %all-to-all-start = ((f32[8,16,48,128]{3,2,1,0:T(8,128)}), f32[8,16,48,128]{3,2,1,0:T(8,128)S(1)}, u32[]{:S(2)}, u32[]{:S(2)}) async-start(f32[8,16,48,128]{3,2,1,0:T(8,128)} %second.2), calls=%async_computation | async-start | bytes 6291456 | tf_op jit(solution)/shard_map/all_to_all | solution.py:398
  31.7 19.7 %third.3 = (f32[48,192,128]{2,1,0:T(8,128)}, f32[48,192,128]{2,1,0:T(8,128)}) custom-call(s32[4]{0:T(128)} %pad_add_fusion.place, f32[6]{0:T(128)} %reshape.22.slopes, f32[64,192,256]{2,1,0:T(8,128)} %v_ref.2, bf16[768,256]{1,0:T(8,128)(2,1)} %constant.82.clone.fw_ref, bf16[768,256]{1,0:T(8,128)(2,1)} %constant.83.clone.iv_ref), custom_call_target="tpu_custom_call" | custom-call | flops 1 | bytes 1 | tf_op jit(solution)/shard_map/third/pallas_call | solution.py:352
  51.4 8.2 %collective-permute-done.1.other_ref = f32[48,192,128]{2,1,0:T(8,128)} collective-permute-done((f32[48,192,128]{2,1,0:T(8,128)}, f32[48,192,128]{2,1,0:T(8,128)}, u32[]{:S(2)}, u32[]{:S(2)}) %collective-permute-start.1) | collective-permute-done | bytes 4718624 | tf_op jit(solution)/shard_map/ppermute | solution.py:400
  59.7 19.7 %second.3 = (f32[48,24,128]{2,1,0:T(8,128)}, f32[48,16,128]{2,1,0:T(8,128)}, f32[48,8,128]{2,1,0:T(8,128)}, f32[48,24,128]{2,1,0:T(8,128)}, f32[48,16,128]{2,1,0...) custom-call(s32[4]{0:T(128)} %pad_add_fusion.place, ...), custom_call_target="tpu_custom_call" | custom-call | flops 1 | bytes 1 | tf_op jit(solution)/shard_map/second/pallas_call | solution.py:372
  79.4 23.3 %all-to-all-done.head_ref = f32[8,16,48,128]{3,2,1,0:T(8,128)S(1)} async-done(((f32[8,16,48,128]{3,2,1,0:T(8,128)}), f32[8,16,48,128]{3,2,1,0:T(8,128)S(1)}, u32[]{:S(2)}, u32[]{:S(2)}) %all-to-all-start) | async-done | bytes 3145760 | tf_op jit(solution)/shard_map/all_to_all | solution.py:398
  102.7 3.8 %collective-permute-start.2 = (f32[48,24,128]{2,1,0:T(8,128)}, f32[48,24,128]{2,1,0:T(8,128)}, u32[]{:S(2)}, u32[]{:S(2)}) collective-permute-start(f32[48,24,128]{2,1,0:T(8,128)} %get-tuple-element.71), channel_id=1, source_target_pairs={{0,10},{2,8},{4,14},{6,12},{8,2},{10,0},{12,6},{14,4},{1,11},{3,9}... | collective-permute-start | bytes 1769480 | tf_op jit(solution)/shard_map/ppermute | solution.py:390
  106.5 0.6 collective-permute-start.17
  107.1 2.3 collective-permute-start.6
  109.4 0.0 collective-permute-start.15
  109.4 47.5 %collective-permute-done.10.refs_4_ = f32[48,24,128]{2,1,0:T(8,128)} collective-permute-done((f32[48,24,128]{2,1,0:T(8,128)}, f32[48,24,128]{2,1,0:T(8,128)}, u32[]{:S(2)}, u32[]{:S(2)}) %collective-permute-start.10) | collective-permute-done | bytes 589856 | tf_op jit(solution)/shard_map/ppermute | solution.py:390
  156.9 1.5 collective-permute-start.11
  158.3 23.8 %collective-permute-done.2.refs_5_ = f32[48,24,128]{2,1,0:T(8,128)} collective-permute-done((f32[48,24,128]{2,1,0:T(8,128)}, f32[48,24,128]{2,1,0:T(8,128)}, u32[]{:S(2)}, u32[]{:S(2)}) %collective-permute-start.2) | collective-permute-done | bytes 589856 | tf_op jit(solution)/shard_map/ppermute | solution.py:390
  182.2 0.6 fusion.4
  182.8 1.9 collective-permute-start.19
  184.7 0.0 collective-permute-done.6.refs_6_
  184.7 10.6 %collective-permute-start.7 = (f32[48,16,128]{2,1,0:T(8,128)}, f32[48,16,128]{2,1,0:T(8,128)S(1)}, u32[]{:S(2)}, u32[]{:S(2)}) collective-permute-start(f32[48,16,128]{2,1,0:T(8,128)} %get-tuple-element.80), channel_id=1, source_target_pairs={{0,10},{2,8},{4,14},{6,12},{8,2},{10,0},{12,6},{14,4},{1,11},{3,9}... | collective-permute-start | bytes 1179656 | tf_op jit(solution)/shard_map/ppermute | solution.py:390
  195.4 0.6 add_multiply_fusion
  196.0 0.6 collective-permute-start.16
  196.5 3.3 %collective-permute-start.12 = (f32[48,16,128]{2,1,0:T(8,128)}, f32[48,16,128]{2,1,0:T(8,128)S(1)}, u32[]{:S(2)}, u32[]{:S(2)}) collective-permute-start(f32[48,16,128]{2,1,0:T(8,128)} %get-tuple-element.90), channel_id=1, source_target_pairs={{0,12},{2,14},{4,8},{6,10},{8,4},{10,6},{12,0},{14,2},{1,13},{3,15... | collective-permute-start | bytes 1179656 | tf_op jit(solution)/shard_map/ppermute | solution.py:390
  199.9 3.9 %fusion = (f32[6,256,8]{2,1,0:T(8,128)}, f32[6,256,8]{2,1,0:T(8,128)}) fusion(f32[6,8]{1,0:T(8,128)S(1)} %add_multiply_fusion, f32[256]{0:T(256)S(1)} %copy-done.17), kind=kLoop, calls=%fused_computation.1 | loop fusion | flops 24576 | bytes 99520 | tf_op jit(solution)/shard_map/sin | solution.py:405
  203.8 0.7 add_multiply_fusion.1
  204.4 38.4 %collective-permute-done.19.refs_4_ = f32[48,16,128]{2,1,0:T(8,128)S(1)} collective-permute-done((f32[48,16,128]{2,1,0:T(8,128)}, f32[48,16,128]{2,1,0:T(8,128)S(1)}, u32[]{:S(2)}, u32[]{:S(2)}) %collective-permute-start.19) | collective-permute-done | bytes 393248 | tf_op jit(solution)/shard_map/ppermute | solution.py:390
  242.8 15.3 %collective-permute-done.7.refs_5_ = f32[48,16,128]{2,1,0:T(8,128)S(1)} collective-permute-done((f32[48,16,128]{2,1,0:T(8,128)}, f32[48,16,128]{2,1,0:T(8,128)S(1)}, u32[]{:S(2)}, u32[]{:S(2)}) %collective-permute-start.7) | collective-permute-done | bytes 393248 | tf_op jit(solution)/shard_map/ppermute | solution.py:390
  258.1 4.5 %collective-permute-start.4 = (f32[48,16,128]{2,1,0:T(8,128)}, f32[48,16,128]{2,1,0:T(8,128)}, u32[]{:S(2)}, u32[]{:S(2)}) collective-permute-start(f32[48,16,128]{2,1,0:T(8,128)} %get-tuple-element.73), channel_id=1, source_target_pairs={{0,4},{2,6},{4,0},{6,2},{8,12},{10,14},{12,8},{14,10},{1,5},{3,7},... | collective-permute-start | bytes 1179656 | tf_op jit(solution)/shard_map/ppermute | solution.py:390
  262.6 1.2 fusion.2
  263.9 13.1 %first.3 = (f32[512,48,128]{2,1,0:T(8,128)}, f32[8,128]{1,0:T(8,128)}) custom-call(s32[4]{0:T(128)} %pad_add_fusion.place, f32[6]{0:T(128)} %reshape.22.slopes, f32[8,16,48,128]{3,2,1,0:T(8,128)} %copy-done, f32[48,24,128]{2,1,0:T(8,128)} %get-tuple-element.98.refs_0_, f32[48,24,128]{2,1,0:T(8,128)} %collective-permute-done.17.refs_1_, ...), custom_call_target="tpu_custom_call" | custom-call | flops 1 | bytes 1 | tf_op jit(solution)/shard_map/first/pallas_call | solution.py:429
  277.0 0.1 collective-permute-start.18
  277.1 1.3 collective-permute-start.13
  278.4 1.3 collective-permute-start.21
  279.7 1.1 collective-permute-start.9
  280.8 2.0 collective-permute-start.5
  282.8 10.6 %first.4 = (f32[512,48,128]{2,1,0:T(8,128)}, f32[8,128]{1,0:T(8,128)}) custom-call(s32[4]{0:T(128)} %pad_add_fusion.place, f32[6]{0:T(128)} %reshape.22.slopes, f32[8,16,48,128]{3,2,1,0:T(8,128)} %copy-done, f32[48,16,128]{2,1,0:T(8,128)} %get-tuple-element.111.refs_0_, f32[48,16,128]{2,1,0:T(8,128)} %copy-done.5, ...), custom_call_target="tpu_custom_call", output_to_operand_aliasing={{0}: (19, {})} | custom-call | flops 1 | bytes 1 | tf_op jit(solution)/shard_map/first/pallas_call | solution.py:429
  293.4 2.2 collective-permute-done.18.refs_4_
  295.7 2.7 collective-permute-start.22
  298.4 6.7 %collective-permute-done.13.refs_5_ = f32[48,8,128]{2,1,0:T(8,128)S(1)} collective-permute-done((f32[48,8,128]{2,1,0:T(8,128)}, f32[48,8,128]{2,1,0:T(8,128)S(1)}, u32[]{:S(2)}, u32[]{:S(2)}) %collective-permute-start.13) | collective-permute-done | bytes 196640 | tf_op jit(solution)/shard_map/ppermute | solution.py:390
  305.2 0.8 collective-permute-done.22.refs_7_
  306.0 5.7 %collective-permute-done.14.refs_3_ = f32[48,8,128]{2,1,0:T(8,128)S(1)} collective-permute-done((f32[48,8,128]{2,1,0:T(8,128)S(1)}, f32[48,8,128]{2,1,0:T(8,128)S(1)}, u32[]{:S(2)}, u32[]{:S(2)}) %collective-permute-start.14) | collective-permute-done | bytes 196640 | tf_op jit(solution)/shard_map/ppermute | solution.py:390
  311.7 0.6 copy-done.15
  312.4 7.0 %first.5 = (f32[512,48,128]{2,1,0:T(8,128)}, f32[8,128]{1,0:T(8,128)}) custom-call(s32[4]{0:T(128)} %pad_add_fusion.place, f32[6]{0:T(128)} %reshape.22.slopes, f32[8,16,48,128]{3,2,1,0:T(8,128)} %copy-done, f32[48,8,128]{2,1,0:T(8,128)} %get-tuple-element.66.refs_0_, f32[48,8,128]{2,1,0:T(8,128)} %copy-done.13, ...), custom_call_target="tpu_custom_call", output_to_operand_aliasing={{0}: (19, {})} | custom-call | flops 1 | bytes 1 | tf_op jit(solution)/shard_map/first/pallas_call | solution.py:429
  (56 shorter events, 0.1 us)
Async XLA Ops:
  10.8 3.7 %collective-permute-start = (f32[16,192,128]{2,1,0:T(8,128)}, f32[16,192,128]{2,1,0:T(8,128)S(1)}, u32[]{:S(2)}, u32[]{:S(2)}) collective-permute-start(f32[16,192,128]{2,1,0:T(8,128)} %get-tuple-element.62), channel_id=1, source_target_pairs={{0,1},{1,0},{2,3},{3,2},{4,5},{5,4},{6,7},{7,6},{8,9},{9,8},{10,11... | collective-permute-start | bytes 4718600 | tf_op jit(solution)/shard_map/ppermute | solution.py:396
  14.5 1.2 copy-start.1
  24.5 78.2 %all-to-all-start = ((f32[8,16,48,128]{3,2,1,0:T(8,128)}), f32[8,16,48,128]{3,2,1,0:T(8,128)S(1)}, u32[]{:S(2)}, u32[]{:S(2)}) async-start(f32[8,16,48,128]{3,2,1,0:T(8,128)} %second.2), calls=%async_computation | async-start | bytes 6291456 | tf_op jit(solution)/shard_map/all_to_all | solution.py:398
  51.4 8.3 %collective-permute-start.1 = (f32[48,192,128]{2,1,0:T(8,128)}, f32[48,192,128]{2,1,0:T(8,128)}, u32[]{:S(2)}, u32[]{:S(2)}) collective-permute-start(f32[48,192,128]{2,1,0:T(8,128)} %get-tuple-element.65), channel_id=1, source_target_pairs={{0,1},{1,0},{2,3},{3,2},{4,5},{5,4},{6,7},{7,6},{8,9},{9,8},{10,11... | collective-permute-start | bytes 14155784 | tf_op jit(solution)/shard_map/ppermute | solution.py:400
  59.7 122.5 %copy-start.16 = (f32[6]{0:T(128)S(1)}, f32[6]{0:T(128)}, u32[]{:S(2)}) copy-start(f32[6]{0:T(128)} %reshape.22.slopes) | copy-start | bytes 76
  59.7 140.2 %copy-start.17 = (f32[256]{0:T(256)S(1)}, f32[256]{0:T(256)}, u32[]{:S(2)}) copy-start(f32[256]{0:T(256)} %constant.95) | copy-start | bytes 3076
  102.7 161.2 %copy-start = (f32[8,16,48,128]{3,2,1,0:T(8,128)}, f32[8,16,48,128]{3,2,1,0:T(8,128)S(1)}, u32[]{:S(2)}) copy-start(f32[8,16,48,128]{3,2,1,0:T(8,128)S(1)} %all-to-all-done.head_ref) | copy-start | bytes 9437188
  102.7 54.2 %collective-permute-start.10 = (f32[48,24,128]{2,1,0:T(8,128)}, f32[48,24,128]{2,1,0:T(8,128)}, u32[]{:S(2)}, u32[]{:S(2)}) collective-permute-start(f32[48,24,128]{2,1,0:T(8,128)} %get-tuple-element.88), channel_id=1, source_target_pairs={{0,8},{2,10},{4,12},{6,14},{8,0},{10,2},{12,4},{14,6},{1,9},{3,11}... | collective-permute-start | bytes 1769480 | tf_op jit(solution)/shard_map/ppermute | solution.py:390
  102.7 79.5 %collective-permute-start.2 = (f32[48,24,128]{2,1,0:T(8,128)}, f32[48,24,128]{2,1,0:T(8,128)}, u32[]{:S(2)}, u32[]{:S(2)}) collective-permute-start(f32[48,24,128]{2,1,0:T(8,128)} %get-tuple-element.71), channel_id=1, source_target_pairs={{0,10},{2,8},{4,14},{6,12},{8,2},{10,0},{12,6},{14,4},{1,11},{3,9}... | collective-permute-start | bytes 1769480 | tf_op jit(solution)/shard_map/ppermute | solution.py:390
  106.5 76.2 %collective-permute-start.17 = (f32[48,24,128]{2,1,0:T(8,128)}, f32[48,24,128]{2,1,0:T(8,128)}, u32[]{:S(2)}, u32[]{:S(2)}) collective-permute-start(f32[48,24,128]{2,1,0:T(8,128)} %get-tuple-element.100), channel_id=1, source_target_pairs={{0,2},{2,0},{4,6},{6,4},{8,10},{10,8},{12,14},{14,12},{1,3},{3,1},... | collective-permute-start | bytes 1769480 | tf_op jit(solution)/shard_map/ppermute | solution.py:390
  107.1 77.6 %collective-permute-start.6 = (f32[48,24,128]{2,1,0:T(8,128)}, f32[48,24,128]{2,1,0:T(8,128)}, u32[]{:S(2)}, u32[]{:S(2)}) collective-permute-start(f32[48,24,128]{2,1,0:T(8,128)} %get-tuple-element.79), channel_id=1, source_target_pairs={{0,12},{2,14},{4,8},{6,10},{8,4},{10,6},{12,0},{14,2},{1,13},{3,15... | collective-permute-start | bytes 1769480 | tf_op jit(solution)/shard_map/ppermute | solution.py:390
  109.4 86.6 %collective-permute-start.15 = (f32[48,24,128]{2,1,0:T(8,128)}, f32[48,24,128]{2,1,0:T(8,128)}, u32[]{:S(2)}, u32[]{:S(2)}) collective-permute-start(f32[48,24,128]{2,1,0:T(8,128)} %get-tuple-element.96), channel_id=1, source_target_pairs={{0,4},{2,6},{4,0},{6,2},{8,12},{10,14},{12,8},{14,10},{1,5},{3,7},... | collective-permute-start | bytes 1769480 | tf_op jit(solution)/shard_map/ppermute | solution.py:390
  156.9 39.7 %collective-permute-start.11 = (f32[48,24,128]{2,1,0:T(8,128)}, f32[48,24,128]{2,1,0:T(8,128)}, u32[]{:S(2)}, u32[]{:S(2)}) collective-permute-start(f32[48,24,128]{2,1,0:T(8,128)} %get-tuple-element.89), channel_id=1, source_target_pairs={{0,14},{2,12},{4,10},{6,8},{8,6},{10,4},{12,2},{14,0},{1,15},{3,13... | collective-permute-start | bytes 1769480 | tf_op jit(solution)/shard_map/ppermute | solution.py:390
  182.2 75.9 %collective-permute-start.3 = (f32[48,24,128]{2,1,0:T(8,128)}, f32[48,24,128]{2,1,0:T(8,128)S(1)}, u32[]{:S(2)}, u32[]{:S(2)}) collective-permute-start(f32[48,24,128]{2,1,0:T(8,128)} %get-tuple-element.72), channel_id=1, source_target_pairs={{0,6},{2,4},{4,2},{6,0},{8,14},{10,12},{12,10},{14,8},{1,7},{3,5},... | collective-permute-start | bytes 1769480 | tf_op jit(solution)/shard_map/ppermute | solution.py:390
  182.8 60.1 %collective-permute-start.19 = (f32[48,16,128]{2,1,0:T(8,128)}, f32[48,16,128]{2,1,0:T(8,128)S(1)}, u32[]{:S(2)}, u32[]{:S(2)}) collective-permute-start(f32[48,16,128]{2,1,0:T(8,128)} %get-tuple-element.107), channel_id=1, source_target_pairs={{0,8},{2,10},{4,12},{6,14},{8,0},{10,2},{12,4},{14,6},{1,9},{3,11}... | collective-permute-start | bytes 1179656 | tf_op jit(solution)/shard_map/ppermute | solution.py:390
  184.7 73.4 %collective-permute-start.7 = (f32[48,16,128]{2,1,0:T(8,128)}, f32[48,16,128]{2,1,0:T(8,128)S(1)}, u32[]{:S(2)}, u32[]{:S(2)}) collective-permute-start(f32[48,16,128]{2,1,0:T(8,128)} %get-tuple-element.80), channel_id=1, source_target_pairs={{0,10},{2,8},{4,14},{6,12},{8,2},{10,0},{12,6},{14,4},{1,11},{3,9}... | collective-permute-start | bytes 1179656 | tf_op jit(solution)/shard_map/ppermute | solution.py:390
  196.0 81.0 %collective-permute-start.16 = (f32[48,16,128]{2,1,0:T(8,128)}, f32[48,16,128]{2,1,0:T(8,128)S(1)}, u32[]{:S(2)}, u32[]{:S(2)}) collective-permute-start(f32[48,16,128]{2,1,0:T(8,128)} %get-tuple-element.97), channel_id=1, source_target_pairs={{0,2},{2,0},{4,6},{6,4},{8,10},{10,8},{12,14},{14,12},{1,3},{3,1},... | collective-permute-start | bytes 1179656 | tf_op jit(solution)/shard_map/ppermute | solution.py:390
  196.5 80.5 %collective-permute-start.12 = (f32[48,16,128]{2,1,0:T(8,128)}, f32[48,16,128]{2,1,0:T(8,128)S(1)}, u32[]{:S(2)}, u32[]{:S(2)}) collective-permute-start(f32[48,16,128]{2,1,0:T(8,128)} %get-tuple-element.90), channel_id=1, source_target_pairs={{0,12},{2,14},{4,8},{6,10},{8,4},{10,6},{12,0},{14,2},{1,13},{3,15... | collective-permute-start | bytes 1179656 | tf_op jit(solution)/shard_map/ppermute | solution.py:390
  242.8 40.0 %copy-start.3 = (f32[48,16,128]{2,1,0:T(8,128)}, f32[48,16,128]{2,1,0:T(8,128)S(1)}, u32[]{:S(2)}) copy-start(f32[48,16,128]{2,1,0:T(8,128)S(1)} %collective-permute-done.19.refs_4_) | copy-start | bytes 1179652
  242.8 35.6 %collective-permute-start.20 = (f32[48,16,128]{2,1,0:T(8,128)}, f32[48,16,128]{2,1,0:T(8,128)S(1)}, u32[]{:S(2)}, u32[]{:S(2)}) collective-permute-start(f32[48,16,128]{2,1,0:T(8,128)} %get-tuple-element.108), channel_id=1, source_target_pairs={{0,14},{2,12},{4,10},{6,8},{8,6},{10,4},{12,2},{14,0},{1,15},{3,13... | collective-permute-start | bytes 1179656 | tf_op jit(solution)/shard_map/ppermute | solution.py:390
  258.1 24.7 %copy-start.4 = (f32[48,16,128]{2,1,0:T(8,128)}, f32[48,16,128]{2,1,0:T(8,128)S(1)}, u32[]{:S(2)}) copy-start(f32[48,16,128]{2,1,0:T(8,128)S(1)} %collective-permute-done.7.refs_5_) | copy-start | bytes 1179652
  258.1 21.6 %collective-permute-start.8 = (f32[48,16,128]{2,1,0:T(8,128)}, f32[48,16,128]{2,1,0:T(8,128)S(1)}, u32[]{:S(2)}, u32[]{:S(2)}) collective-permute-start(f32[48,16,128]{2,1,0:T(8,128)} %get-tuple-element.81), channel_id=1, source_target_pairs={{0,6},{2,4},{4,2},{6,0},{8,14},{10,12},{12,10},{14,8},{1,7},{3,5},... | collective-permute-start | bytes 1179656 | tf_op jit(solution)/shard_map/ppermute | solution.py:390
  258.1 5.8 %copy-start.2 = (f32[48,24,128]{2,1,0:T(8,128)}, f32[48,24,128]{2,1,0:T(8,128)S(1)}, u32[]{:S(2)}) copy-start(f32[48,24,128]{2,1,0:T(8,128)S(1)} %collective-permute-done.3.refs_3_) | copy-start | bytes 1769476
  258.1 22.7 %collective-permute-start.4 = (f32[48,16,128]{2,1,0:T(8,128)}, f32[48,16,128]{2,1,0:T(8,128)}, u32[]{:S(2)}, u32[]{:S(2)}) collective-permute-start(f32[48,16,128]{2,1,0:T(8,128)} %get-tuple-element.73), channel_id=1, source_target_pairs={{0,4},{2,6},{4,0},{6,2},{8,12},{10,14},{12,8},{14,10},{1,5},{3,7},... | collective-permute-start | bytes 1179656 | tf_op jit(solution)/shard_map/ppermute | solution.py:390
  277.0 5.8 %copy-start.5 = (f32[48,16,128]{2,1,0:T(8,128)}, f32[48,16,128]{2,1,0:T(8,128)S(1)}, u32[]{:S(2)}) copy-start(f32[48,16,128]{2,1,0:T(8,128)S(1)} %collective-permute-done.16.refs_1_) | copy-start | bytes 1179652
  277.0 18.7 %collective-permute-start.18 = (f32[48,8,128]{2,1,0:T(8,128)}, f32[48,8,128]{2,1,0:T(8,128)S(1)}, u32[]{:S(2)}, u32[]{:S(2)}) collective-permute-start(f32[48,8,128]{2,1,0:T(8,128)} %get-tuple-element.103), channel_id=1, source_target_pairs={{0,8},{2,10},{4,12},{6,14},{8,0},{10,2},{12,4},{14,6},{1,9},{3,11}... | collective-permute-start | bytes 589832 | tf_op jit(solution)/shard_map/ppermute | solution.py:390
  277.1 5.7 %copy-start.6 = (f32[48,16,128]{2,1,0:T(8,128)}, f32[48,16,128]{2,1,0:T(8,128)S(1)}, u32[]{:S(2)}) copy-start(f32[48,16,128]{2,1,0:T(8,128)S(1)} %collective-permute-done.12.refs_6_) | copy-start | bytes 1179652
  277.1 28.0 %collective-permute-start.13 = (f32[48,8,128]{2,1,0:T(8,128)}, f32[48,8,128]{2,1,0:T(8,128)S(1)}, u32[]{:S(2)}, u32[]{:S(2)}) collective-permute-start(f32[48,8,128]{2,1,0:T(8,128)} %get-tuple-element.91), channel_id=1, source_target_pairs={{0,10},{2,8},{4,14},{6,12},{8,2},{10,0},{12,6},{14,4},{1,11},{3,9}... | collective-permute-start | bytes 589832 | tf_op jit(solution)/shard_map/ppermute | solution.py:390
  278.4 4.4 %copy-start.7 = (f32[48,16,128]{2,1,0:T(8,128)}, f32[48,16,128]{2,1,0:T(8,128)S(1)}, u32[]{:S(2)}) copy-start(f32[48,16,128]{2,1,0:T(8,128)S(1)} %collective-permute-done.20.refs_7_) | copy-start | bytes 1179652
  278.4 26.7 %collective-permute-start.21 = (f32[48,8,128]{2,1,0:T(8,128)}, f32[48,8,128]{2,1,0:T(8,128)S(1)}, u32[]{:S(2)}, u32[]{:S(2)}) collective-permute-start(f32[48,8,128]{2,1,0:T(8,128)} %get-tuple-element.109), channel_id=1, source_target_pairs={{0,12},{2,14},{4,8},{6,10},{8,4},{10,6},{12,0},{14,2},{1,13},{3,15... | collective-permute-start | bytes 589832 | tf_op jit(solution)/shard_map/ppermute | solution.py:390
  279.7 3.1 copy-start.8
  279.7 25.4 %collective-permute-start.9 = (f32[48,8,128]{2,1,0:T(8,128)}, f32[48,8,128]{2,1,0:T(8,128)S(1)}, u32[]{:S(2)}, u32[]{:S(2)}) collective-permute-start(f32[48,8,128]{2,1,0:T(8,128)} %get-tuple-element.82), channel_id=1, source_target_pairs={{0,4},{2,6},{4,0},{6,2},{8,12},{10,14},{12,8},{14,10},{1,5},{3,7},... | collective-permute-start | bytes 589832 | tf_op jit(solution)/shard_map/ppermute | solution.py:390
  280.8 24.3 %collective-permute-start.5 = (f32[48,8,128]{2,1,0:T(8,128)}, f32[48,8,128]{2,1,0:T(8,128)S(1)}, u32[]{:S(2)}, u32[]{:S(2)}) collective-permute-start(f32[48,8,128]{2,1,0:T(8,128)} %get-tuple-element.74), channel_id=1, source_target_pairs={{0,2},{2,0},{4,6},{6,4},{8,10},{10,8},{12,14},{14,12},{1,3},{3,1},... | collective-permute-start | bytes 589832 | tf_op jit(solution)/shard_map/ppermute | solution.py:390
  282.8 12.9 %copy-start.19 = (f32[48,8,128]{2,1,0:T(8,128)S(1)}, f32[48,8,128]{2,1,0:T(8,128)}, u32[]{:S(2)}) copy-start(f32[48,8,128]{2,1,0:T(8,128)} %get-tuple-element.114) | copy-start | bytes 589828
  282.8 22.3 %copy-start.18 = (f32[48,8,128]{2,1,0:T(8,128)S(1)}, f32[48,8,128]{2,1,0:T(8,128)}, u32[]{:S(2)}) copy-start(f32[48,8,128]{2,1,0:T(8,128)} %get-tuple-element.92) | copy-start | bytes 589828
  295.7 16.0 %copy-start.9 = (f32[48,8,128]{2,1,0:T(8,128)}, f32[48,8,128]{2,1,0:T(8,128)S(1)}, u32[]{:S(2)}) copy-start(f32[48,8,128]{2,1,0:T(8,128)S(1)} %collective-permute-done.18.refs_4_) | copy-start | bytes 589828
  295.7 10.3 %collective-permute-start.22 = (f32[48,8,128]{2,1,0:T(8,128)S(1)}, f32[48,8,128]{2,1,0:T(8,128)S(1)}, u32[]{:S(2)}, u32[]{:S(2)}) collective-permute-start(f32[48,8,128]{2,1,0:T(8,128)S(1)} %copy-done.19), channel_id=1, source_target_pairs={{0,14},{2,12},{4,10},{6,8},{8,6},{10,4},{12,2},{14,0},{1,15},{3,13... | collective-permute-start | bytes 589832 | tf_op jit(solution)/shard_map/ppermute | solution.py:390
  305.1 6.6 %copy-start.10 = (f32[48,8,128]{2,1,0:T(8,128)}, f32[48,8,128]{2,1,0:T(8,128)S(1)}, u32[]{:S(2)}) copy-start(f32[48,8,128]{2,1,0:T(8,128)S(1)} %collective-permute-done.13.refs_5_) | copy-start | bytes 589828
  305.1 6.6 %collective-permute-start.14 = (f32[48,8,128]{2,1,0:T(8,128)S(1)}, f32[48,8,128]{2,1,0:T(8,128)S(1)}, u32[]{:S(2)}, u32[]{:S(2)}) collective-permute-start(f32[48,8,128]{2,1,0:T(8,128)S(1)} %copy-done.18), channel_id=1, source_target_pairs={{0,6},{2,4},{4,2},{6,0},{8,14},{10,12},{12,10},{14,8},{1,7},{3,5},... | collective-permute-start | bytes 589832 | tf_op jit(solution)/shard_map/ppermute | solution.py:390
  305.1 6.6 %copy-start.11 = (f32[48,8,128]{2,1,0:T(8,128)}, f32[48,8,128]{2,1,0:T(8,128)S(1)}, u32[]{:S(2)}) copy-start(f32[48,8,128]{2,1,0:T(8,128)S(1)} %collective-permute-done.21.refs_6_) | copy-start | bytes 589828
  305.2 6.5 %copy-start.12 = (f32[48,8,128]{2,1,0:T(8,128)}, f32[48,8,128]{2,1,0:T(8,128)S(1)}, u32[]{:S(2)}) copy-start(f32[48,8,128]{2,1,0:T(8,128)S(1)} %collective-permute-done.9.refs_2_) | copy-start | bytes 589828
  305.2 6.5 %copy-start.13 = (f32[48,8,128]{2,1,0:T(8,128)}, f32[48,8,128]{2,1,0:T(8,128)S(1)}, u32[]{:S(2)}) copy-start(f32[48,8,128]{2,1,0:T(8,128)S(1)} %collective-permute-done.5.refs_1_) | copy-start | bytes 589828
  306.0 5.8 %copy-start.14 = (f32[48,8,128]{2,1,0:T(8,128)}, f32[48,8,128]{2,1,0:T(8,128)S(1)}, u32[]{:S(2)}) copy-start(f32[48,8,128]{2,1,0:T(8,128)S(1)} %collective-permute-done.22.refs_7_) | copy-start | bytes 589828
  311.7 0.7 copy-start.15

commit v2 on v1

--- a/solution.py
+++ b/solution.py
@@ -14,9 +14,10 @@
 F32 = jnp.float32
 BF16 = jnp.bfloat16
 VMEM_LIMIT = 58 * 1024 * 1024
-XB = 4
+XB = 8
 HEAD = 2
 CHUNKS = (3, 2, 1)
+GATES = (2,)
 WINDOW = 5
 
 
@@ -123,30 +124,24 @@
 
         padded = c1_scr.shape[0]
         c1_scr[...], s1_scr[...] = turns(
-            frequency(padded), offsets(padded, place[1] + x0, full[0], slopes[4]), n
+            frequency(padded), offsets(padded, place[1] + x0, full[0], slopes[2, 0]), n
         )
-        c2_scr[...], s2_scr[...] = turns(frequency(ny), offsets(ny, place[2] * ny, full[1], slopes[5]), n)
-
-    v = v_ref[...].reshape(xb * ny, n)
-    high, low = split(v)
-    spectrum = dot(jnp.concatenate([high, low, high], 1), fw_ref[...])
+        c2_scr[...], s2_scr[...] = turns(frequency(ny), offsets(ny, place[2] * ny, full[1], slopes[2, 1]), n)
+
     first = iota((ny, half), 1) == 0
-    parts = []
+    mine = place[2] == 0
     for x in range(xb):
-        rows = slice(x * ny, (x + 1) * ny)
+        high, low = split(v_ref[x])
+        spectrum = dot(jnp.concatenate([high, low, high], 1), fw_ref[...])
         at = pl.ds(step * xb + x, 1)
         c, s = turn(
-            spectrum[rows, :half], spectrum[rows, half:],
-            c1_scr[at, :], s1_scr[at, :], c2_scr[...], s2_scr[...], first,
+            spectrum[:, :half], spectrum[:, half:], c1_scr[at, :], s1_scr[at, :], c2_scr[...], s2_scr[...], first
         )
-        parts.append(jnp.concatenate([c, s], 1))
-    high, low = split(jnp.concatenate(parts, 0))
-    back = dot(jnp.concatenate([high, low, high], 1), iv_ref[...])
-    lower = back[:, :half].reshape(xb, ny, half)
-    upper = back[:, half:].reshape(xb, ny, half)
-    mine = place[2] == 0
-    own_ref[...] = jnp.where(mine, lower, upper)
-    other_ref[...] = jnp.where(mine, upper, lower)
+        high, low = split(jnp.concatenate([c, s], 1))
+        back = dot(jnp.concatenate([high, low, high], 1), iv_ref[...])
+        lower, upper = back[:, :half], back[:, half:]
+        own_ref[x] = jnp.where(mine, lower, upper)
+        other_ref[x] = jnp.where(mine, upper, lower)
 
 
 def second_kernel(
@@ -170,13 +165,13 @@
             return jnp.where(r == 0, half, f).astype(F32)
 
         lanes = iota((half, 128), 1)
-        c1, s1 = turns(frequency(128), slopes[2] * ((lanes + (place[1] + x0)).astype(F32) - full[0] / 2), n)
+        c1, s1 = turns(frequency(128), slopes[1, 0] * ((lanes + (place[1] + x0)).astype(F32) - full[0] / 2), n)
         for b in range(c1_scr.shape[0]):
             c1_scr[b] = c1[:, b * xb : (b + 1) * xb]
             s1_scr[b] = s1[:, b * xb : (b + 1) * xb]
         lanes = iota((half, nk), 1)
         c2_scr[...], s2_scr[...] = turns(
-            frequency(nk), slopes[3] * ((lanes + place[2] * nk).astype(F32) - full[2] / 2), n
+            frequency(nk), slopes[1, 1] * ((lanes + place[2] * nk).astype(F32) - full[2] / 2), n
         )
 
     col_sign = (1 - 2 * place[2]).astype(F32)
@@ -334,7 +329,7 @@
     heights = tuple(part * sixths // 6 for sixths in CHUNKS) if part % 48 == 0 else (part,)
     rows = 8 if part % 8 == 0 else part
     place = jnp.stack([row_place % blocks, row_place * xl, col_place, row_place // blocks]).astype(jnp.int32)
-    slopes = factors.reshape(-1)
+    slopes = factors
 
     z_forward, z_inverse = (rhs3(matrix) for matrix in direct_matrices(nz))
     y_mats = [lhs3(matrix) for matrix in split_matrices(ny)]
@@ -376,7 +371,7 @@
         )(place, slopes, own, other, *y_mats)
 
     sent = []
-    order = [d for pair in zip(range(blocks, row_count), range(blocks)) for d in pair if d]
+    order = [d for pair in zip([*range(1, blocks), 0], range(blocks, row_count)) for d in pair if d]
 
     def after(value, *others):
         return lax.optimization_barrier((value, *others))[0]
@@ -409,8 +404,8 @@
 
     late = after(slopes, outs[0])
     fx = frequencies_split(nx)
-    xc1, xs1 = waves(fx[None, :, None], (late[0] * centred(part, row_place * part, ny)).reshape(-1, 1, rows), nx)
-    xc2, xs2 = waves(fx[:, None], (late[1] * centred(nk, col_place * nk, nz))[None, :], nx)
+    xc1, xs1 = waves(fx[None, :, None], (late[0, 0] * centred(part, row_place * part, ny)).reshape(-1, 1, rows), nx)
+    xc2, xs2 = waves(fx[:, None], (late[0, 1] * centred(nk, col_place * nk, nz))[None, :], nx)
 
     def first(y0, height, got, result, token):
         base = y0 // rows
@@ -435,7 +430,7 @@
         )(place, slopes, *ins)
 
     result, token, tokens, y0 = None, None, [], 0
-    got = [spread(pieces[0], {i: head for i in range(WINDOW)})]
+    got = [spread(pieces[0], {i: head for i in GATES})]
     for c, height in enumerate(heights):
         ahead = c + 1
         if ahead < len(heights):

time: 321 us -> 313 us (0.975)
  Pallas kernels: 87.8 us -> 77.4 us
  waiting for transfers between devices: 175 us -> 185 us
  starting transfers between devices: 45.2 us -> 39.4 us
    all_to_all x1, waiting for transfers between devices: 23.3 us -> 53.4 us  [body(): head = lax.all_to_all(head, 'row', 0, 0, tiled=True)]
    ppermute x21, waiting for transfers between devices: 141 us -> 120 us  [spread(): lax.ppermute(after(pieces[d], *others), 'row', [(i, i ^ d) for i in range...]
    pallas_call x2, Pallas kernels: 28.5 us -> 21.7 us  [third(): call(functools.partial(third_kernel, x0, size, full), size // xb, [pl.Blo...]
    ppermute x21, starting transfers between devices: 37.5 us -> 31.7 us  [spread(): lax.ppermute(after(pieces[d], *others), 'row', [(i, i ^ d) for i in range...]
    pallas_call x2, Pallas kernels: 28.6 us -> 24.8 us  [second(): call(functools.partial(second_kernel, x0, heights, part, full), size // x...]
  transfers between devices with their start and end apart: 24 -> 24, of which waited for: 11 -> 11; matrix products, arithmetic and copies ran while one was open for 2% -> 2% of each run, Pallas kernels for 20% -> 18%
where the time goes in v2:
time: 313 us
  waiting for transfers between devices  185 us (59%)
  Pallas kernels  77.4 us (25%)
  starting transfers between devices  39.4 us (13%)
  other arithmetic  7.64 us (2%)
  local copies, waits for them, and re-layouts  3.29 us (1%)
    ppermute x21, waiting for transfers between devices, spread(): lax.ppermute(after(pieces[d], *others), 'row', [(i, i ^ d) for i in range...  120 us
    all_to_all x1, waiting for transfers between devices, body(): head = lax.all_to_all(head, 'row', 0, 0, tiled=True)  53.4 us
    ppermute x21, starting transfers between devices, spread(): lax.ppermute(after(pieces[d], *others), 'row', [(i, i ^ d) for i in range...  31.7 us
    pallas_call x3, Pallas kernels, first(): call(first_kernel, height // rows, specs, [pl.BlockSpec((nx, rows, nk), l...  30.9 us
    pallas_call x2, Pallas kernels, second(): call(functools.partial(second_kernel, x0, heights, part, full), size // x...  24.8 us
    pallas_call x2, Pallas kernels, third(): call(functools.partial(third_kernel, x0, size, full), size // xb, [pl.Blo...  21.7 us
    ppermute x1, waiting for transfers between devices, body(): lax.ppermute(other, 'col', swap)  8.25 us
    all_to_all x1, starting transfers between devices, body(): head = lax.all_to_all(head, 'row', 0, 0, tiled=True)  7.2 us
  transfers between devices with their start and end apart: 24, of which 11 were waited for; matrix products, arithmetic and copies ran while one was open for 2% of the time, Pallas kernels for 18%

profile of v2, /device:TPU:0, one launch (start us, length us, event | category | flops | bytes accessed | tf_op | source)
XLA Modules:
  0.0 312.8 jit_solution(15589353504022647568)
XLA Ops:
  0.0 0.8 copy.17
  0.8 0.6 multiply_tan_fusion.slopes
  1.4 0.6 pad_add_fusion.place
  2.0 7.2 %third.2 = (f32[16,192,128]{2,1,0:T(8,128)}, f32[16,192,128]{2,1,0:T(8,128)}) custom-call(s32[4]{0:T(128)} %pad_add_fusion.place, f32[3,2]{1,0:T(4,128)} %multiply_tan_fusion.slopes, f32[64,192,256]{2,1,0:T(8,128)} %v_ref.2, bf16[768,256]{1,0:T(8,128)(2,1)} %constant.82.clone.fw_ref, bf16[768,256]{1,0:T(8,128)(2,1)} %constant.83.clone.iv_ref), custom_call_target="tpu_custom_call" | custom-call | flops 1 | bytes 1 | tf_op jit(solution)/shard_map/third/pallas_call | solution.py:347
  9.1 0.5 collective-permute-start
  9.6 3.2 %collective-permute-done.other_ref = f32[16,192,128]{2,1,0:T(8,128)S(1)} collective-permute-done((f32[16,192,128]{2,1,0:T(8,128)}, f32[16,192,128]{2,1,0:T(8,128)S(1)}, u32[]{:S(2)}, u32[]{:S(2)}) %collective-permute-start) | collective-permute-done | bytes 1572896 | tf_op jit(solution)/shard_map/ppermute | solution.py:391
  12.8 1.2 copy-done.1
  14.0 8.1 %second.2 = f32[8,16,48,128]{3,2,1,0:T(8,128)} custom-call(s32[4]{0:T(128)} %pad_add_fusion.place, f32[3,2]{1,0:T(4,128)} %multiply_tan_fusion.slopes, f32[16,192,128]{2,1,0:T(8,128)} %get-tuple-element.57.own_ref, f32[16,192,128]{2,1,0:T(8,128)} %copy-done.1, bf16[192,576]{1,0:T(8,128)(2,1)} %constant.84.clone.fe_ref, ...), custom_call_target="tpu_custom_call" | custom-call | flops 1 | bytes 1 | tf_op jit(solution)/shard_map/second/pallas_call | solution.py:367
  22.1 7.2 %all-to-all-start = ((f32[8,16,48,128]{3,2,1,0:T(8,128)}), f32[8,16,48,128]{3,2,1,0:T(8,128)S(1)}, u32[]{:S(2)}, u32[]{:S(2)}) async-start(f32[8,16,48,128]{3,2,1,0:T(8,128)} %second.2), calls=%async_computation | async-start | bytes 6291456 | tf_op jit(solution)/shard_map/all_to_all | solution.py:393
  29.3 14.6 %third.3 = (f32[48,192,128]{2,1,0:T(8,128)}, f32[48,192,128]{2,1,0:T(8,128)}) custom-call(s32[4]{0:T(128)} %pad_add_fusion.place, f32[3,2]{1,0:T(4,128)} %multiply_tan_fusion.slopes, f32[64,192,256]{2,1,0:T(8,128)} %v_ref.2, bf16[768,256]{1,0:T(8,128)(2,1)} %constant.82.clone.fw_ref, bf16[768,256]{1,0:T(8,128)(2,1)} %constant.83.clone.iv_ref), custom_call_target="tpu_custom_call" | custom-call | flops 1 | bytes 1 | tf_op jit(solution)/shard_map/third/pallas_call | solution.py:347
  43.9 0.0 collective-permute-start.1
  43.9 8.2 %collective-permute-done.1.other_ref = f32[48,192,128]{2,1,0:T(8,128)} collective-permute-done((f32[48,192,128]{2,1,0:T(8,128)}, f32[48,192,128]{2,1,0:T(8,128)}, u32[]{:S(2)}, u32[]{:S(2)}) %collective-permute-start.1) | collective-permute-done | bytes 4718624 | tf_op jit(solution)/shard_map/ppermute | solution.py:395
  52.2 16.6 %second.3 = (f32[48,24,128]{2,1,0:T(8,128)}, f32[48,16,128]{2,1,0:T(8,128)}, f32[48,8,128]{2,1,0:T(8,128)}, f32[48,24,128]{2,1,0:T(8,128)}, f32[48,16,128]{2,1,0...) custom-call(s32[4]{0:T(128)} %pad_add_fusion.place, ...), custom_call_target="tpu_custom_call" | custom-call | flops 1 | bytes 1 | tf_op jit(solution)/shard_map/second/pallas_call | solution.py:367
  68.8 2.1 collective-permute-start.4
  70.9 2.4 collective-permute-start.6
  73.2 0.1 collective-permute-start.7
  73.3 53.4 %all-to-all-done.head_ref = f32[8,16,48,128]{3,2,1,0:T(8,128)S(1)} async-done(((f32[8,16,48,128]{3,2,1,0:T(8,128)}), f32[8,16,48,128]{3,2,1,0:T(8,128)S(1)}, u32[]{:S(2)}, u32[]{:S(2)}) %all-to-all-start) | async-done | bytes 3145760 | tf_op jit(solution)/shard_map/all_to_all | solution.py:393
  126.7 2.9 collective-permute-start.2
  129.6 0.5 collective-permute-start.8
  130.1 9.4 %collective-permute-done.6.refs_4_ = f32[48,24,128]{2,1,0:T(8,128)} collective-permute-done((f32[48,24,128]{2,1,0:T(8,128)}, f32[48,24,128]{2,1,0:T(8,128)}, u32[]{:S(2)}, u32[]{:S(2)}) %collective-permute-start.6) | collective-permute-done | bytes 589856 | tf_op jit(solution)/shard_map/ppermute | solution.py:385
  139.5 1.4 collective-permute-start.9
  140.9 0.6 fusion.4
  141.5 11.5 %collective-permute-done.7.refs_5_ = f32[48,24,128]{2,1,0:T(8,128)} collective-permute-done((f32[48,24,128]{2,1,0:T(8,128)}, f32[48,24,128]{2,1,0:T(8,128)}, u32[]{:S(2)}, u32[]{:S(2)}) %collective-permute-start.7) | collective-permute-done | bytes 589856 | tf_op jit(solution)/shard_map/ppermute | solution.py:385
  153.0 36.1 %collective-permute-done.5.refs_2_ = f32[48,24,128]{2,1,0:T(8,128)} collective-permute-done((f32[48,24,128]{2,1,0:T(8,128)}, f32[48,24,128]{2,1,0:T(8,128)}, u32[]{:S(2)}, u32[]{:S(2)}) %collective-permute-start.5) | collective-permute-done | bytes 589856 | tf_op jit(solution)/shard_map/ppermute | solution.py:385
  189.0 1.5 collective-permute-start.18
  190.5 0.7 add_multiply_fusion
  191.2 11.4 %collective-permute-done.2.refs_3_ = f32[48,24,128]{2,1,0:T(8,128)} collective-permute-done((f32[48,24,128]{2,1,0:T(8,128)}, f32[48,24,128]{2,1,0:T(8,128)}, u32[]{:S(2)}, u32[]{:S(2)}) %collective-permute-start.2) | collective-permute-done | bytes 589856 | tf_op jit(solution)/shard_map/ppermute | solution.py:385
  202.6 2.8 collective-permute-start.16
  205.4 3.9 %fusion = (f32[6,256,8]{2,1,0:T(8,128)}, f32[6,256,8]{2,1,0:T(8,128)}) fusion(f32[6,8]{1,0:T(8,128)S(1)} %add_multiply_fusion, f32[256]{0:T(256)S(1)} %copy-done.16), kind=kLoop, calls=%fused_computation.1 | loop fusion | flops 24576 | bytes 99520 | tf_op jit(solution)/shard_map/sin | solution.py:400
  209.3 0.7 add_multiply_fusion.1
  209.9 18.0 %collective-permute-done.13.refs_4_ = f32[48,16,128]{2,1,0:T(8,128)S(1)} collective-permute-done((f32[48,16,128]{2,1,0:T(8,128)}, f32[48,16,128]{2,1,0:T(8,128)S(1)}, u32[]{:S(2)}, u32[]{:S(2)}) %collective-permute-start.13) | collective-permute-done | bytes 393248 | tf_op jit(solution)/shard_map/ppermute | solution.py:385
  227.9 1.4 collective-permute-start.14
  229.3 0.0 collective-permute-done.9.refs_7_
  229.3 0.0 collective-permute-start.11
  229.4 3.3 %collective-permute-start.19 = (f32[48,16,128]{2,1,0:T(8,128)}, f32[48,16,128]{2,1,0:T(8,128)}, u32[]{:S(2)}, u32[]{:S(2)}) collective-permute-start(f32[48,16,128]{2,1,0:T(8,128)} %get-tuple-element.98), channel_id=1, source_target_pairs={{0,12},{2,14},{4,8},{6,10},{8,4},{10,6},{12,0},{14,2},{1,13},{3,15... | collective-permute-start | bytes 1179656 | tf_op jit(solution)/shard_map/ppermute | solution.py:385
  232.7 1.3 fusion.2
  233.9 12.1 %collective-permute-done.16.refs_5_ = f32[48,16,128]{2,1,0:T(8,128)S(1)} collective-permute-done((f32[48,16,128]{2,1,0:T(8,128)}, f32[48,16,128]{2,1,0:T(8,128)S(1)}, u32[]{:S(2)}, u32[]{:S(2)}) %collective-permute-start.16) | collective-permute-done | bytes 393248 | tf_op jit(solution)/shard_map/ppermute | solution.py:385
  246.0 13.2 %first.3 = (f32[512,48,128]{2,1,0:T(8,128)}, f32[8,128]{1,0:T(8,128)}) custom-call(s32[4]{0:T(128)} %pad_add_fusion.place, f32[3,2]{1,0:T(4,128)} %multiply_tan_fusion.slopes, f32[8,16,48,128]{3,2,1,0:T(8,128)} %copy-done, f32[48,24,128]{2,1,0:T(8,128)} %get-tuple-element.67.refs_0_, f32[48,24,128]{2,1,0:T(8,128)} %collective-permute-done.4.refs_1_, ...), custom_call_target="tpu_custom_call" | custom-call | flops 1 | bytes 1 | tf_op jit(solution)/shard_map/first/pallas_call | solution.py:424
  259.2 0.3 collective-permute-start.10
  259.6 8.0 %collective-permute-start.15 = (f32[48,8,128]{2,1,0:T(8,128)}, f32[48,8,128]{2,1,0:T(8,128)S(1)}, u32[]{:S(2)}, u32[]{:S(2)}) collective-permute-start(f32[48,8,128]{2,1,0:T(8,128)} %get-tuple-element.89), channel_id=1, source_target_pairs={{0,6},{2,4},{4,2},{6,0},{8,14},{10,12},{12,10},{14,8},{1,7},{3,5},... | collective-permute-start | bytes 589832 | tf_op jit(solution)/shard_map/ppermute | solution.py:385
  267.6 10.3 %collective-permute-done.17.refs_4_ = f32[48,8,128]{2,1,0:T(8,128)} collective-permute-done((f32[48,8,128]{2,1,0:T(8,128)}, f32[48,8,128]{2,1,0:T(8,128)}, u32[]{:S(2)}, u32[]{:S(2)}) %collective-permute-start.17) | collective-permute-done | bytes 196640 | tf_op jit(solution)/shard_map/ppermute | solution.py:385
  277.9 4.9 %collective-permute-start.22 = (f32[48,8,128]{2,1,0:T(8,128)}, f32[48,8,128]{2,1,0:T(8,128)S(1)}, u32[]{:S(2)}, u32[]{:S(2)}) collective-permute-start(f32[48,8,128]{2,1,0:T(8,128)} %get-tuple-element.106), channel_id=1, source_target_pairs={{0,14},{2,12},{4,10},{6,8},{8,6},{10,4},{12,2},{14,0},{1,15},{3,13... | collective-permute-start | bytes 589832 | tf_op jit(solution)/shard_map/ppermute | solution.py:385
  282.9 10.6 %first.4 = (f32[512,48,128]{2,1,0:T(8,128)}, f32[8,128]{1,0:T(8,128)}) custom-call(s32[4]{0:T(128)} %pad_add_fusion.place, f32[3,2]{1,0:T(4,128)} %multiply_tan_fusion.slopes, f32[8,16,48,128]{3,2,1,0:T(8,128)} %copy-done, f32[48,16,128]{2,1,0:T(8,128)} %get-tuple-element.101.refs_0_, f32[48,16,128]{2,1,0:T(8,128)} %copy-done.4, ...), custom_call_target="tpu_custom_call", output_to_operand_aliasing={{0}: (19, {})} | custom-call | flops 1 | bytes 1 | tf_op jit(solution)/shard_map/first/pallas_call | solution.py:424
  293.6 0.1 collective-permute-start.21
  293.7 11.3 %collective-permute-done.20.refs_5_ = f32[48,8,128]{2,1,0:T(8,128)S(1)} collective-permute-done((f32[48,8,128]{2,1,0:T(8,128)}, f32[48,8,128]{2,1,0:T(8,128)S(1)}, u32[]{:S(2)}, u32[]{:S(2)}) %collective-permute-start.20) | collective-permute-done | bytes 196640 | tf_op jit(solution)/shard_map/ppermute | solution.py:385
  305.0 0.6 copy-done.13
  305.7 0.1 copy-done.14
  305.8 7.1 %first.5 = (f32[512,48,128]{2,1,0:T(8,128)}, f32[8,128]{1,0:T(8,128)}) custom-call(s32[4]{0:T(128)} %pad_add_fusion.place, f32[3,2]{1,0:T(4,128)} %multiply_tan_fusion.slopes, f32[8,16,48,128]{3,2,1,0:T(8,128)} %copy-done, f32[48,8,128]{2,1,0:T(8,128)} %get-tuple-element.62.refs_0_, f32[48,8,128]{2,1,0:T(8,128)} %copy-done.9, ...), custom_call_target="tpu_custom_call", output_to_operand_aliasing={{0}: (19, {})} | custom-call | flops 1 | bytes 1 | tf_op jit(solution)/shard_map/first/pallas_call | solution.py:424
  (51 shorter events, 0.1 us)
Async XLA Ops:
  9.1 3.7 %collective-permute-start = (f32[16,192,128]{2,1,0:T(8,128)}, f32[16,192,128]{2,1,0:T(8,128)S(1)}, u32[]{:S(2)}, u32[]{:S(2)}) collective-permute-start(f32[16,192,128]{2,1,0:T(8,128)} %get-tuple-element.58), channel_id=1, source_target_pairs={{0,1},{1,0},{2,3},{3,2},{4,5},{5,4},{6,7},{7,6},{8,9},{9,8},{10,11... | collective-permute-start | bytes 4718600 | tf_op jit(solution)/shard_map/ppermute | solution.py:391
  12.8 1.2 copy-start.1
  22.1 104.6 %all-to-all-start = ((f32[8,16,48,128]{3,2,1,0:T(8,128)}), f32[8,16,48,128]{3,2,1,0:T(8,128)S(1)}, u32[]{:S(2)}, u32[]{:S(2)}) async-start(f32[8,16,48,128]{3,2,1,0:T(8,128)} %second.2), calls=%async_computation | async-start | bytes 6291456 | tf_op jit(solution)/shard_map/all_to_all | solution.py:393
  43.9 8.3 %collective-permute-start.1 = (f32[48,192,128]{2,1,0:T(8,128)}, f32[48,192,128]{2,1,0:T(8,128)}, u32[]{:S(2)}, u32[]{:S(2)}) collective-permute-start(f32[48,192,128]{2,1,0:T(8,128)} %get-tuple-element.61), channel_id=1, source_target_pairs={{0,1},{1,0},{2,3},{3,2},{4,5},{5,4},{6,7},{7,6},{8,9},{9,8},{10,11... | collective-permute-start | bytes 14155784 | tf_op jit(solution)/shard_map/ppermute | solution.py:395
  52.2 88.8 %copy-start.15 = (f32[3,2]{1,0:T(4,128)S(1)}, f32[3,2]{1,0:T(4,128)}, u32[]{:S(2)}) copy-start(f32[3,2]{1,0:T(4,128)} %multiply_tan_fusion.slopes) | copy-start | bytes 76
  52.2 153.2 %copy-start.16 = (f32[256]{0:T(256)S(1)}, f32[256]{0:T(256)}, u32[]{:S(2)}) copy-start(f32[256]{0:T(256)} %constant.95) | copy-start | bytes 3076
  68.8 60.8 %collective-permute-start.4 = (f32[48,24,128]{2,1,0:T(8,128)}, f32[48,24,128]{2,1,0:T(8,128)}, u32[]{:S(2)}, u32[]{:S(2)}) collective-permute-start(f32[48,24,128]{2,1,0:T(8,128)} %get-tuple-element.68), channel_id=1, source_target_pairs={{0,2},{2,0},{4,6},{6,4},{8,10},{10,8},{12,14},{14,12},{1,3},{3,1},... | collective-permute-start | bytes 1769480 | tf_op jit(solution)/shard_map/ppermute | solution.py:385
  70.9 68.7 %collective-permute-start.6 = (f32[48,24,128]{2,1,0:T(8,128)}, f32[48,24,128]{2,1,0:T(8,128)}, u32[]{:S(2)}, u32[]{:S(2)}) collective-permute-start(f32[48,24,128]{2,1,0:T(8,128)} %get-tuple-element.71), channel_id=1, source_target_pairs={{0,8},{2,10},{4,12},{6,14},{8,0},{10,2},{12,4},{14,6},{1,9},{3,11}... | collective-permute-start | bytes 1769480 | tf_op jit(solution)/shard_map/ppermute | solution.py:385
  73.2 79.7 %collective-permute-start.7 = (f32[48,24,128]{2,1,0:T(8,128)}, f32[48,24,128]{2,1,0:T(8,128)}, u32[]{:S(2)}, u32[]{:S(2)}) collective-permute-start(f32[48,24,128]{2,1,0:T(8,128)} %get-tuple-element.72), channel_id=1, source_target_pairs={{0,10},{2,8},{4,14},{6,12},{8,2},{10,0},{12,6},{14,4},{1,11},{3,9}... | collective-permute-start | bytes 1769480 | tf_op jit(solution)/shard_map/ppermute | solution.py:385
  126.7 119.3 %copy-start = (f32[8,16,48,128]{3,2,1,0:T(8,128)}, f32[8,16,48,128]{3,2,1,0:T(8,128)S(1)}, u32[]{:S(2)}) copy-start(f32[8,16,48,128]{3,2,1,0:T(8,128)S(1)} %all-to-all-done.head_ref) | copy-start | bytes 9437188
  126.7 62.3 %collective-permute-start.5 = (f32[48,24,128]{2,1,0:T(8,128)}, f32[48,24,128]{2,1,0:T(8,128)}, u32[]{:S(2)}, u32[]{:S(2)}) collective-permute-start(f32[48,24,128]{2,1,0:T(8,128)} %get-tuple-element.70), channel_id=1, source_target_pairs={{0,4},{2,6},{4,0},{6,2},{8,12},{10,14},{12,8},{14,10},{1,5},{3,7},... | collective-permute-start | bytes 1769480 | tf_op jit(solution)/shard_map/ppermute | solution.py:385
  126.7 75.9 %collective-permute-start.2 = (f32[48,24,128]{2,1,0:T(8,128)}, f32[48,24,128]{2,1,0:T(8,128)}, u32[]{:S(2)}, u32[]{:S(2)}) collective-permute-start(f32[48,24,128]{2,1,0:T(8,128)} %get-tuple-element.65), channel_id=1, source_target_pairs={{0,6},{2,4},{4,2},{6,0},{8,14},{10,12},{12,10},{14,8},{1,7},{3,5},... | collective-permute-start | bytes 1769480 | tf_op jit(solution)/shard_map/ppermute | solution.py:385
  129.6 73.0 %collective-permute-start.8 = (f32[48,24,128]{2,1,0:T(8,128)}, f32[48,24,128]{2,1,0:T(8,128)}, u32[]{:S(2)}, u32[]{:S(2)}) collective-permute-start(f32[48,24,128]{2,1,0:T(8,128)} %get-tuple-element.74), channel_id=1, source_target_pairs={{0,12},{2,14},{4,8},{6,10},{8,4},{10,6},{12,0},{14,2},{1,13},{3,15... | collective-permute-start | bytes 1769480 | tf_op jit(solution)/shard_map/ppermute | solution.py:385
  139.5 89.8 %collective-permute-start.9 = (f32[48,24,128]{2,1,0:T(8,128)}, f32[48,24,128]{2,1,0:T(8,128)S(1)}, u32[]{:S(2)}, u32[]{:S(2)}) collective-permute-start(f32[48,24,128]{2,1,0:T(8,128)} %get-tuple-element.76), channel_id=1, source_target_pairs={{0,14},{2,12},{4,10},{6,8},{8,6},{10,4},{12,2},{14,0},{1,15},{3,13... | collective-permute-start | bytes 1769480 | tf_op jit(solution)/shard_map/ppermute | solution.py:385
  152.9 75.0 %collective-permute-start.13 = (f32[48,16,128]{2,1,0:T(8,128)}, f32[48,16,128]{2,1,0:T(8,128)S(1)}, u32[]{:S(2)}, u32[]{:S(2)}) collective-permute-start(f32[48,16,128]{2,1,0:T(8,128)} %get-tuple-element.87), channel_id=1, source_target_pairs={{0,8},{2,10},{4,12},{6,14},{8,0},{10,2},{12,4},{14,6},{1,9},{3,11}... | collective-permute-start | bytes 1179656 | tf_op jit(solution)/shard_map/ppermute | solution.py:385
  189.0 40.3 %collective-permute-start.18 = (f32[48,16,128]{2,1,0:T(8,128)}, f32[48,16,128]{2,1,0:T(8,128)S(1)}, u32[]{:S(2)}, u32[]{:S(2)}) collective-permute-start(f32[48,16,128]{2,1,0:T(8,128)} %get-tuple-element.97), channel_id=1, source_target_pairs={{0,2},{2,0},{4,6},{6,4},{8,10},{10,8},{12,14},{14,12},{1,3},{3,1},... | collective-permute-start | bytes 1179656 | tf_op jit(solution)/shard_map/ppermute | solution.py:385
  202.6 56.7 %collective-permute-start.3 = (f32[48,16,128]{2,1,0:T(8,128)}, f32[48,16,128]{2,1,0:T(8,128)S(1)}, u32[]{:S(2)}, u32[]{:S(2)}) collective-permute-start(f32[48,16,128]{2,1,0:T(8,128)} %get-tuple-element.66), channel_id=1, source_target_pairs={{0,4},{2,6},{4,0},{6,2},{8,12},{10,14},{12,8},{14,10},{1,5},{3,7},... | collective-permute-start | bytes 1179656 | tf_op jit(solution)/shard_map/ppermute | solution.py:385
  202.6 43.5 %collective-permute-start.16 = (f32[48,16,128]{2,1,0:T(8,128)}, f32[48,16,128]{2,1,0:T(8,128)S(1)}, u32[]{:S(2)}, u32[]{:S(2)}) collective-permute-start(f32[48,16,128]{2,1,0:T(8,128)} %get-tuple-element.92), channel_id=1, source_target_pairs={{0,10},{2,8},{4,14},{6,12},{8,2},{10,0},{12,6},{14,4},{1,11},{3,9}... | collective-permute-start | bytes 1179656 | tf_op jit(solution)/shard_map/ppermute | solution.py:385
  227.9 54.9 %copy-start.3 = (f32[48,16,128]{2,1,0:T(8,128)}, f32[48,16,128]{2,1,0:T(8,128)S(1)}, u32[]{:S(2)}) copy-start(f32[48,16,128]{2,1,0:T(8,128)S(1)} %collective-permute-done.13.refs_4_) | copy-start | bytes 1179652
  227.9 31.6 %collective-permute-start.14 = (f32[48,16,128]{2,1,0:T(8,128)}, f32[48,16,128]{2,1,0:T(8,128)S(1)}, u32[]{:S(2)}, u32[]{:S(2)}) collective-permute-start(f32[48,16,128]{2,1,0:T(8,128)} %get-tuple-element.88), channel_id=1, source_target_pairs={{0,14},{2,12},{4,10},{6,8},{8,6},{10,4},{12,2},{14,0},{1,15},{3,13... | collective-permute-start | bytes 1179656 | tf_op jit(solution)/shard_map/ppermute | solution.py:385
  229.3 16.7 %copy-start.2 = (f32[48,24,128]{2,1,0:T(8,128)}, f32[48,24,128]{2,1,0:T(8,128)S(1)}, u32[]{:S(2)}) copy-start(f32[48,24,128]{2,1,0:T(8,128)S(1)} %collective-permute-done.9.refs_7_) | copy-start | bytes 1769476
  229.3 38.3 %collective-permute-start.11 = (f32[48,16,128]{2,1,0:T(8,128)}, f32[48,16,128]{2,1,0:T(8,128)S(1)}, u32[]{:S(2)}, u32[]{:S(2)}) collective-permute-start(f32[48,16,128]{2,1,0:T(8,128)} %get-tuple-element.82), channel_id=1, source_target_pairs={{0,6},{2,4},{4,2},{6,0},{8,14},{10,12},{12,10},{14,8},{1,7},{3,5},... | collective-permute-start | bytes 1179656 | tf_op jit(solution)/shard_map/ppermute | solution.py:385
  229.3 29.9 %copy-start.4 = (f32[48,16,128]{2,1,0:T(8,128)}, f32[48,16,128]{2,1,0:T(8,128)S(1)}, u32[]{:S(2)}) copy-start(f32[48,16,128]{2,1,0:T(8,128)S(1)} %collective-permute-done.18.refs_1_) | copy-start | bytes 1179652
  229.4 53.5 %collective-permute-start.19 = (f32[48,16,128]{2,1,0:T(8,128)}, f32[48,16,128]{2,1,0:T(8,128)}, u32[]{:S(2)}, u32[]{:S(2)}) collective-permute-start(f32[48,16,128]{2,1,0:T(8,128)} %get-tuple-element.98), channel_id=1, source_target_pairs={{0,12},{2,14},{4,8},{6,10},{8,4},{10,6},{12,0},{14,2},{1,13},{3,15... | collective-permute-start | bytes 1179656 | tf_op jit(solution)/shard_map/ppermute | solution.py:385
  246.0 13.2 %copy-start.6 = (f32[48,16,128]{2,1,0:T(8,128)}, f32[48,16,128]{2,1,0:T(8,128)S(1)}, u32[]{:S(2)}) copy-start(f32[48,16,128]{2,1,0:T(8,128)S(1)} %collective-permute-done.16.refs_5_) | copy-start | bytes 1179652
  246.0 31.9 %collective-permute-start.17 = (f32[48,8,128]{2,1,0:T(8,128)}, f32[48,8,128]{2,1,0:T(8,128)}, u32[]{:S(2)}, u32[]{:S(2)}) collective-permute-start(f32[48,8,128]{2,1,0:T(8,128)} %get-tuple-element.93), channel_id=1, source_target_pairs={{0,8},{2,10},{4,12},{6,14},{8,0},{10,2},{12,4},{14,6},{1,9},{3,11}... | collective-permute-start | bytes 589832 | tf_op jit(solution)/shard_map/ppermute | solution.py:385
  259.2 23.6 %copy-start.5 = (f32[48,16,128]{2,1,0:T(8,128)}, f32[48,16,128]{2,1,0:T(8,128)S(1)}, u32[]{:S(2)}) copy-start(f32[48,16,128]{2,1,0:T(8,128)S(1)} %collective-permute-done.3.refs_2_) | copy-start | bytes 1179652
  259.2 34.3 %collective-permute-start.10 = (f32[48,8,128]{2,1,0:T(8,128)}, f32[48,8,128]{2,1,0:T(8,128)S(1)}, u32[]{:S(2)}, u32[]{:S(2)}) collective-permute-start(f32[48,8,128]{2,1,0:T(8,128)} %get-tuple-element.79), channel_id=1, source_target_pairs={{0,2},{2,0},{4,6},{6,4},{8,10},{10,8},{12,14},{14,12},{1,3},{3,1},... | collective-permute-start | bytes 589832 | tf_op jit(solution)/shard_map/ppermute | solution.py:385
  259.6 23.3 %copy-start.7 = (f32[48,16,128]{2,1,0:T(8,128)}, f32[48,16,128]{2,1,0:T(8,128)S(1)}, u32[]{:S(2)}) copy-start(f32[48,16,128]{2,1,0:T(8,128)S(1)} %collective-permute-done.14.refs_7_) | copy-start | bytes 1179652
  259.6 34.1 %collective-permute-start.15 = (f32[48,8,128]{2,1,0:T(8,128)}, f32[48,8,128]{2,1,0:T(8,128)S(1)}, u32[]{:S(2)}, u32[]{:S(2)}) collective-permute-start(f32[48,8,128]{2,1,0:T(8,128)} %get-tuple-element.89), channel_id=1, source_target_pairs={{0,6},{2,4},{4,2},{6,0},{8,14},{10,12},{12,10},{14,8},{1,7},{3,5},... | collective-permute-start | bytes 589832 | tf_op jit(solution)/shard_map/ppermute | solution.py:385
  267.6 15.3 %copy-start.8 = (f32[48,16,128]{2,1,0:T(8,128)}, f32[48,16,128]{2,1,0:T(8,128)S(1)}, u32[]{:S(2)}) copy-start(f32[48,16,128]{2,1,0:T(8,128)S(1)} %collective-permute-done.11.refs_3_) | copy-start | bytes 1179652
  267.6 26.1 %collective-permute-start.12 = (f32[48,8,128]{2,1,0:T(8,128)}, f32[48,8,128]{2,1,0:T(8,128)S(1)}, u32[]{:S(2)}, u32[]{:S(2)}) collective-permute-start(f32[48,8,128]{2,1,0:T(8,128)} %get-tuple-element.83), channel_id=1, source_target_pairs={{0,4},{2,6},{4,0},{6,2},{8,12},{10,14},{12,8},{14,10},{1,5},{3,7},... | collective-permute-start | bytes 589832 | tf_op jit(solution)/shard_map/ppermute | solution.py:385
  277.9 15.8 %collective-permute-start.22 = (f32[48,8,128]{2,1,0:T(8,128)}, f32[48,8,128]{2,1,0:T(8,128)S(1)}, u32[]{:S(2)}, u32[]{:S(2)}) collective-permute-start(f32[48,8,128]{2,1,0:T(8,128)} %get-tuple-element.106), channel_id=1, source_target_pairs={{0,14},{2,12},{4,10},{6,8},{8,6},{10,4},{12,2},{14,0},{1,15},{3,13... | collective-permute-start | bytes 589832 | tf_op jit(solution)/shard_map/ppermute | solution.py:385
  282.8 22.2 %collective-permute-start.20 = (f32[48,8,128]{2,1,0:T(8,128)}, f32[48,8,128]{2,1,0:T(8,128)S(1)}, u32[]{:S(2)}, u32[]{:S(2)}) collective-permute-start(f32[48,8,128]{2,1,0:T(8,128)} %get-tuple-element.99), channel_id=1, source_target_pairs={{0,10},{2,8},{4,14},{6,12},{8,2},{10,0},{12,6},{14,4},{1,11},{3,9}... | collective-permute-start | bytes 589832 | tf_op jit(solution)/shard_map/ppermute | solution.py:385
  282.9 10.7 %copy-start.17 = (f32[48,8,128]{2,1,0:T(8,128)S(1)}, f32[48,8,128]{2,1,0:T(8,128)}, u32[]{:S(2)}) copy-start(f32[48,8,128]{2,1,0:T(8,128)} %get-tuple-element.104) | copy-start | bytes 589828
  293.5 11.5 %copy-start.9 = (f32[48,8,128]{2,1,0:T(8,128)}, f32[48,8,128]{2,1,0:T(8,128)S(1)}, u32[]{:S(2)}) copy-start(f32[48,8,128]{2,1,0:T(8,128)S(1)} %collective-permute-done.10.refs_1_) | copy-start | bytes 589828
  293.6 11.5 %collective-permute-start.21 = (f32[48,8,128]{2,1,0:T(8,128)S(1)}, f32[48,8,128]{2,1,0:T(8,128)S(1)}, u32[]{:S(2)}, u32[]{:S(2)}) collective-permute-start(f32[48,8,128]{2,1,0:T(8,128)S(1)} %copy-done.17), channel_id=1, source_target_pairs={{0,12},{2,14},{4,8},{6,10},{8,4},{10,6},{12,0},{14,2},{1,13},{3,15... | collective-permute-start | bytes 589832 | tf_op jit(solution)/shard_map/ppermute | solution.py:385
  293.7 11.4 %copy-start.10 = (f32[48,8,128]{2,1,0:T(8,128)}, f32[48,8,128]{2,1,0:T(8,128)S(1)}, u32[]{:S(2)}) copy-start(f32[48,8,128]{2,1,0:T(8,128)S(1)} %collective-permute-done.15.refs_3_) | copy-start | bytes 589828
  293.7 11.4 %copy-start.11 = (f32[48,8,128]{2,1,0:T(8,128)}, f32[48,8,128]{2,1,0:T(8,128)S(1)}, u32[]{:S(2)}) copy-start(f32[48,8,128]{2,1,0:T(8,128)S(1)} %collective-permute-done.12.refs_2_) | copy-start | bytes 589828
  293.7 11.4 %copy-start.12 = (f32[48,8,128]{2,1,0:T(8,128)}, f32[48,8,128]{2,1,0:T(8,128)S(1)}, u32[]{:S(2)}) copy-start(f32[48,8,128]{2,1,0:T(8,128)S(1)} %collective-permute-done.22.refs_7_) | copy-start | bytes 589828
  305.0 0.7 copy-start.13
  305.0 0.7 copy-start.14

commit v3 on v2

--- a/solution.py
+++ b/solution.py
@@ -376,7 +376,7 @@
     def after(value, *others):
         return lax.optimization_barrier((value, *others))[0]
 
-    def spread(pieces, gates=None):
+    def spread(pieces, order, gates=None):
         got = [pieces[0]] + [None] * (row_count - 1)
         for i, d in enumerate(order):
             others = list(sent[-WINDOW:][:1]) if len(sent) >= WINDOW else []
@@ -430,7 +430,8 @@
         )(place, slopes, *ins)
 
     result, token, tokens, y0 = None, None, [], 0
-    got = [spread(pieces[0], {i: head for i in GATES})]
+    last = [*order[:-3], *order[-3:-1][::-1], order[-1]]
+    got = [spread(pieces[0], order, {i: head for i in GATES})]
     for c, height in enumerate(heights):
         ahead = c + 1
         if ahead < len(heights):
@@ -441,7 +442,7 @@
                 result, token = first(y0, height, got[c], result, token)
                 tokens.append(token)
                 gates[len(order) - 2] = token
-            got.append(spread(pieces[ahead], gates))
+            got.append(spread(pieces[ahead], last if ahead == len(heights) - 1 else order, gates))
         if len(tokens) == c:
             result, token = first(y0, height, got[c], result, token)
             tokens.append(token)

time: 313 us -> 317 us (1.013)
  starting transfers between devices: 39.4 us -> 46 us
    ppermute x21, starting transfers between devices: 31.7 us -> 38.3 us  [spread(): lax.ppermute(after(pieces[d], *others), 'row', [(i, i ^ d) for i in range...]
    ppermute x21, waiting for transfers between devices: 120 us -> 117 us  [spread(): lax.ppermute(after(pieces[d], *others), 'row', [(i, i ^ d) for i in range...]
  transfers between devices with their start and end apart: 24 -> 24, of which waited for: 11 -> 13; matrix products, arithmetic and copies ran while one was open for 2% -> 2% of each run, Pallas kernels for 18% -> 17%
where the time goes in v3:
time: 317 us; the launch traced here: 316 us
  waiting for transfers between devices  182 us (57%)
  Pallas kernels  77.4 us (24%)
  starting transfers between devices  46 us (15%)
  other arithmetic  7.64 us (2%)
  local copies, waits for them, and re-layouts  3.24 us (1%)
    ppermute x21, waiting for transfers between devices, spread(): lax.ppermute(after(pieces[d], *others), 'row', [(i, i ^ d) for i in range...  117 us
    all_to_all x1, waiting for transfers between devices, body(): head = lax.all_to_all(head, 'row', 0, 0, tiled=True)  53.4 us
    ppermute x21, starting transfers between devices, spread(): lax.ppermute(after(pieces[d], *others), 'row', [(i, i ^ d) for i in range...  38.3 us
    pallas_call x3, Pallas kernels, first(): call(first_kernel, height // rows, specs, [pl.BlockSpec((nx, rows, nk), l...  30.9 us
    pallas_call x2, Pallas kernels, second(): call(functools.partial(second_kernel, x0, heights, part, full), size // x...  24.8 us
    pallas_call x2, Pallas kernels, third(): call(functools.partial(third_kernel, x0, size, full), size // xb, [pl.Blo...  21.7 us
    ppermute x1, waiting for transfers between devices, body(): lax.ppermute(other, 'col', swap)  8.25 us
    all_to_all x1, starting transfers between devices, body(): head = lax.all_to_all(head, 'row', 0, 0, tiled=True)  7.2 us
  transfers between devices with their start and end apart: 24, of which 13 were waited for; matrix products, arithmetic and copies ran while one was open for 2% of the time, Pallas kernels for 17%

profile of v3, /device:TPU:0, one launch (start us, length us, event | category | flops | bytes accessed | tf_op | source)
XLA Modules:
  0.0 316.1 jit_solution(7670284687663843235)
XLA Ops:
  0.0 0.8 copy.17
  0.8 0.6 multiply_tan_fusion.slopes
  1.4 0.6 pad_add_fusion.place
  2.0 7.2 %third.2 = (f32[16,192,128]{2,1,0:T(8,128)}, f32[16,192,128]{2,1,0:T(8,128)}) custom-call(s32[4]{0:T(128)} %pad_add_fusion.place, f32[3,2]{1,0:T(4,128)} %multiply_tan_fusion.slopes, f32[64,192,256]{2,1,0:T(8,128)} %v_ref.2, bf16[768,256]{1,0:T(8,128)(2,1)} %constant.82.clone.fw_ref, bf16[768,256]{1,0:T(8,128)(2,1)} %constant.83.clone.iv_ref), custom_call_target="tpu_custom_call" | custom-call | flops 1 | bytes 1 | tf_op jit(solution)/shard_map/third/pallas_call | solution.py:347
  9.1 0.5 collective-permute-start
  9.6 3.2 %collective-permute-done.other_ref = f32[16,192,128]{2,1,0:T(8,128)S(1)} collective-permute-done((f32[16,192,128]{2,1,0:T(8,128)}, f32[16,192,128]{2,1,0:T(8,128)S(1)}, u32[]{:S(2)}, u32[]{:S(2)}) %collective-permute-start) | collective-permute-done | bytes 1572896 | tf_op jit(solution)/shard_map/ppermute | solution.py:391
  12.8 1.2 copy-done.1
  14.0 8.1 %second.2 = f32[8,16,48,128]{3,2,1,0:T(8,128)} custom-call(s32[4]{0:T(128)} %pad_add_fusion.place, f32[3,2]{1,0:T(4,128)} %multiply_tan_fusion.slopes, f32[16,192,128]{2,1,0:T(8,128)} %get-tuple-element.57.own_ref, f32[16,192,128]{2,1,0:T(8,128)} %copy-done.1, bf16[192,576]{1,0:T(8,128)(2,1)} %constant.84.clone.fe_ref, ...), custom_call_target="tpu_custom_call" | custom-call | flops 1 | bytes 1 | tf_op jit(solution)/shard_map/second/pallas_call | solution.py:367
  22.1 7.2 %all-to-all-start = ((f32[8,16,48,128]{3,2,1,0:T(8,128)}), f32[8,16,48,128]{3,2,1,0:T(8,128)S(1)}, u32[]{:S(2)}, u32[]{:S(2)}) async-start(f32[8,16,48,128]{3,2,1,0:T(8,128)} %second.2), calls=%async_computation | async-start | bytes 6291456 | tf_op jit(solution)/shard_map/all_to_all | solution.py:393
  29.3 14.6 %third.3 = (f32[48,192,128]{2,1,0:T(8,128)}, f32[48,192,128]{2,1,0:T(8,128)}) custom-call(s32[4]{0:T(128)} %pad_add_fusion.place, f32[3,2]{1,0:T(4,128)} %multiply_tan_fusion.slopes, f32[64,192,256]{2,1,0:T(8,128)} %v_ref.2, bf16[768,256]{1,0:T(8,128)(2,1)} %constant.82.clone.fw_ref, bf16[768,256]{1,0:T(8,128)(2,1)} %constant.83.clone.iv_ref), custom_call_target="tpu_custom_call" | custom-call | flops 1 | bytes 1 | tf_op jit(solution)/shard_map/third/pallas_call | solution.py:347
  43.9 8.2 %collective-permute-done.1.other_ref = f32[48,192,128]{2,1,0:T(8,128)} collective-permute-done((f32[48,192,128]{2,1,0:T(8,128)}, f32[48,192,128]{2,1,0:T(8,128)}, u32[]{:S(2)}, u32[]{:S(2)}) %collective-permute-start.1) | collective-permute-done | bytes 4718624 | tf_op jit(solution)/shard_map/ppermute | solution.py:395
  52.2 16.6 %second.3 = (f32[48,24,128]{2,1,0:T(8,128)}, f32[48,16,128]{2,1,0:T(8,128)}, f32[48,8,128]{2,1,0:T(8,128)}, f32[48,24,128]{2,1,0:T(8,128)}, f32[48,16,128]{2,1,0...) custom-call(s32[4]{0:T(128)} %pad_add_fusion.place, ...), custom_call_target="tpu_custom_call" | custom-call | flops 1 | bytes 1 | tf_op jit(solution)/shard_map/second/pallas_call | solution.py:367
  68.8 2.1 collective-permute-start.4
  70.9 2.4 collective-permute-start.6
  73.2 0.1 collective-permute-start.7
  73.3 53.4 %all-to-all-done.head_ref = f32[8,16,48,128]{3,2,1,0:T(8,128)S(1)} async-done(((f32[8,16,48,128]{3,2,1,0:T(8,128)}), f32[8,16,48,128]{3,2,1,0:T(8,128)S(1)}, u32[]{:S(2)}, u32[]{:S(2)}) %all-to-all-start) | async-done | bytes 3145760 | tf_op jit(solution)/shard_map/all_to_all | solution.py:393
  126.7 2.9 collective-permute-start.2
  129.6 0.5 collective-permute-start.8
  130.1 9.4 %collective-permute-done.6.refs_4_ = f32[48,24,128]{2,1,0:T(8,128)} collective-permute-done((f32[48,24,128]{2,1,0:T(8,128)}, f32[48,24,128]{2,1,0:T(8,128)}, u32[]{:S(2)}, u32[]{:S(2)}) %collective-permute-start.6) | collective-permute-done | bytes 589856 | tf_op jit(solution)/shard_map/ppermute | solution.py:385
  139.5 1.4 collective-permute-start.9
  140.9 0.6 fusion.4
  141.5 11.5 %collective-permute-done.7.refs_5_ = f32[48,24,128]{2,1,0:T(8,128)} collective-permute-done((f32[48,24,128]{2,1,0:T(8,128)}, f32[48,24,128]{2,1,0:T(8,128)}, u32[]{:S(2)}, u32[]{:S(2)}) %collective-permute-start.7) | collective-permute-done | bytes 589856 | tf_op jit(solution)/shard_map/ppermute | solution.py:385
  153.0 36.1 %collective-permute-done.5.refs_2_ = f32[48,24,128]{2,1,0:T(8,128)} collective-permute-done((f32[48,24,128]{2,1,0:T(8,128)}, f32[48,24,128]{2,1,0:T(8,128)}, u32[]{:S(2)}, u32[]{:S(2)}) %collective-permute-start.5) | collective-permute-done | bytes 589856 | tf_op jit(solution)/shard_map/ppermute | solution.py:385
  189.0 1.5 collective-permute-start.13
  190.5 0.7 add_multiply_fusion
  191.2 11.4 %collective-permute-done.2.refs_3_ = f32[48,24,128]{2,1,0:T(8,128)} collective-permute-done((f32[48,24,128]{2,1,0:T(8,128)}, f32[48,24,128]{2,1,0:T(8,128)}, u32[]{:S(2)}, u32[]{:S(2)}) %collective-permute-start.2) | collective-permute-done | bytes 589856 | tf_op jit(solution)/shard_map/ppermute | solution.py:385
  202.6 2.8 collective-permute-start.15
  205.4 3.9 %fusion = (f32[6,256,8]{2,1,0:T(8,128)}, f32[6,256,8]{2,1,0:T(8,128)}) fusion(f32[6,8]{1,0:T(8,128)S(1)} %add_multiply_fusion, f32[256]{0:T(256)S(1)} %copy-done.16), kind=kLoop, calls=%fused_computation.1 | loop fusion | flops 24576 | bytes 99520 | tf_op jit(solution)/shard_map/sin | solution.py:400
  209.3 0.7 add_multiply_fusion.1
  209.9 18.0 %collective-permute-done.14.refs_4_ = f32[48,16,128]{2,1,0:T(8,128)S(1)} collective-permute-done((f32[48,16,128]{2,1,0:T(8,128)}, f32[48,16,128]{2,1,0:T(8,128)S(1)}, u32[]{:S(2)}, u32[]{:S(2)}) %collective-permute-start.14) | collective-permute-done | bytes 393248 | tf_op jit(solution)/shard_map/ppermute | solution.py:385
  227.9 1.4 collective-permute-start.17
  229.3 0.0 collective-permute-start.11
  229.4 3.3 %collective-permute-start.16 = (f32[48,16,128]{2,1,0:T(8,128)}, f32[48,16,128]{2,1,0:T(8,128)}, u32[]{:S(2)}, u32[]{:S(2)}) collective-permute-start(f32[48,16,128]{2,1,0:T(8,128)} %get-tuple-element.93), channel_id=1, source_target_pairs={{0,12},{2,14},{4,8},{6,10},{8,4},{10,6},{12,0},{14,2},{1,13},{3,15... | collective-permute-start | bytes 1179656 | tf_op jit(solution)/shard_map/ppermute | solution.py:385
  232.7 1.3 fusion.2
  233.9 12.1 %collective-permute-done.15.refs_5_ = f32[48,16,128]{2,1,0:T(8,128)S(1)} collective-permute-done((f32[48,16,128]{2,1,0:T(8,128)}, f32[48,16,128]{2,1,0:T(8,128)S(1)}, u32[]{:S(2)}, u32[]{:S(2)}) %collective-permute-start.15) | collective-permute-done | bytes 393248 | tf_op jit(solution)/shard_map/ppermute | solution.py:385
  246.0 13.2 %first.3 = (f32[512,48,128]{2,1,0:T(8,128)}, f32[8,128]{1,0:T(8,128)}) custom-call(s32[4]{0:T(128)} %pad_add_fusion.place, f32[3,2]{1,0:T(4,128)} %multiply_tan_fusion.slopes, f32[8,16,48,128]{3,2,1,0:T(8,128)} %copy-done, f32[48,24,128]{2,1,0:T(8,128)} %get-tuple-element.67.refs_0_, f32[48,24,128]{2,1,0:T(8,128)} %collective-permute-done.4.refs_1_, ...), custom_call_target="tpu_custom_call" | custom-call | flops 1 | bytes 1 | tf_op jit(solution)/shard_map/first/pallas_call | solution.py:424
  259.2 0.3 collective-permute-start.10
  259.6 1.3 collective-permute-start.21
  260.9 0.7 collective-permute-done.11.refs_3_
  261.6 12.3 %collective-permute-start.12 = (f32[48,8,128]{2,1,0:T(8,128)}, f32[48,8,128]{2,1,0:T(8,128)S(1)}, u32[]{:S(2)}, u32[]{:S(2)}) collective-permute-start(f32[48,8,128]{2,1,0:T(8,128)} %get-tuple-element.83), channel_id=1, source_target_pairs={{0,4},{2,6},{4,0},{6,2},{8,12},{10,14},{12,8},{14,10},{1,5},{3,7},... | collective-permute-start | bytes 589832 | tf_op jit(solution)/shard_map/ppermute | solution.py:385
  273.9 9.2 %collective-permute-done.19.refs_4_ = f32[48,8,128]{2,1,0:T(8,128)} collective-permute-done((f32[48,8,128]{2,1,0:T(8,128)}, f32[48,8,128]{2,1,0:T(8,128)}, u32[]{:S(2)}, u32[]{:S(2)}) %collective-permute-start.19) | collective-permute-done | bytes 196640 | tf_op jit(solution)/shard_map/ppermute | solution.py:385
  283.1 3.9 %collective-permute-start.22 = (f32[48,8,128]{2,1,0:T(8,128)}, f32[48,8,128]{2,1,0:T(8,128)S(1)}, u32[]{:S(2)}, u32[]{:S(2)}) collective-permute-start(f32[48,8,128]{2,1,0:T(8,128)} %get-tuple-element.106), channel_id=1, source_target_pairs={{0,14},{2,12},{4,10},{6,8},{8,6},{10,4},{12,2},{14,0},{1,15},{3,13... | collective-permute-start | bytes 589832 | tf_op jit(solution)/shard_map/ppermute | solution.py:385
  287.0 10.6 %first.4 = (f32[512,48,128]{2,1,0:T(8,128)}, f32[8,128]{1,0:T(8,128)}) custom-call(s32[4]{0:T(128)} %pad_add_fusion.place, f32[3,2]{1,0:T(4,128)} %multiply_tan_fusion.slopes, f32[8,16,48,128]{3,2,1,0:T(8,128)} %copy-done, f32[48,16,128]{2,1,0:T(8,128)} %get-tuple-element.85.refs_0_, f32[48,16,128]{2,1,0:T(8,128)} %copy-done.4, ...), custom_call_target="tpu_custom_call", output_to_operand_aliasing={{0}: (19, {})} | custom-call | flops 1 | bytes 1 | tf_op jit(solution)/shard_map/first/pallas_call | solution.py:424
  297.7 2.1 collective-permute-start.18
  299.9 4.3 %collective-permute-done.20.refs_5_ = f32[48,8,128]{2,1,0:T(8,128)S(1)} collective-permute-done((f32[48,8,128]{2,1,0:T(8,128)}, f32[48,8,128]{2,1,0:T(8,128)S(1)}, u32[]{:S(2)}, u32[]{:S(2)}) %collective-permute-start.20) | collective-permute-done | bytes 196640 | tf_op jit(solution)/shard_map/ppermute | solution.py:385
  304.2 4.1 %collective-permute-done.18.refs_3_ = f32[48,8,128]{2,1,0:T(8,128)S(1)} collective-permute-done((f32[48,8,128]{2,1,0:T(8,128)S(1)}, f32[48,8,128]{2,1,0:T(8,128)S(1)}, u32[]{:S(2)}, u32[]{:S(2)}) %collective-permute-start.18) | collective-permute-done | bytes 196640 | tf_op jit(solution)/shard_map/ppermute | solution.py:385
  308.4 0.7 copy-done.14
  309.0 7.1 %first.5 = (f32[512,48,128]{2,1,0:T(8,128)}, f32[8,128]{1,0:T(8,128)}) custom-call(s32[4]{0:T(128)} %pad_add_fusion.place, f32[3,2]{1,0:T(4,128)} %multiply_tan_fusion.slopes, f32[8,16,48,128]{3,2,1,0:T(8,128)} %copy-done, f32[48,8,128]{2,1,0:T(8,128)} %get-tuple-element.62.refs_0_, f32[48,8,128]{2,1,0:T(8,128)} %copy-done.9, ...), custom_call_target="tpu_custom_call", output_to_operand_aliasing={{0}: (19, {})} | custom-call | flops 1 | bytes 1 | tf_op jit(solution)/shard_map/first/pallas_call | solution.py:424
  (51 shorter events, 0.1 us)
Async XLA Ops:
  9.1 3.7 %collective-permute-start = (f32[16,192,128]{2,1,0:T(8,128)}, f32[16,192,128]{2,1,0:T(8,128)S(1)}, u32[]{:S(2)}, u32[]{:S(2)}) collective-permute-start(f32[16,192,128]{2,1,0:T(8,128)} %get-tuple-element.58), channel_id=1, source_target_pairs={{0,1},{1,0},{2,3},{3,2},{4,5},{5,4},{6,7},{7,6},{8,9},{9,8},{10,11... | collective-permute-start | bytes 4718600 | tf_op jit(solution)/shard_map/ppermute | solution.py:391
  12.8 1.2 copy-start.1
  22.1 104.6 %all-to-all-start = ((f32[8,16,48,128]{3,2,1,0:T(8,128)}), f32[8,16,48,128]{3,2,1,0:T(8,128)S(1)}, u32[]{:S(2)}, u32[]{:S(2)}) async-start(f32[8,16,48,128]{3,2,1,0:T(8,128)} %second.2), calls=%async_computation | async-start | bytes 6291456 | tf_op jit(solution)/shard_map/all_to_all | solution.py:393
  43.9 8.3 %collective-permute-start.1 = (f32[48,192,128]{2,1,0:T(8,128)}, f32[48,192,128]{2,1,0:T(8,128)}, u32[]{:S(2)}, u32[]{:S(2)}) collective-permute-start(f32[48,192,128]{2,1,0:T(8,128)} %get-tuple-element.61), channel_id=1, source_target_pairs={{0,1},{1,0},{2,3},{3,2},{4,5},{5,4},{6,7},{7,6},{8,9},{9,8},{10,11... | collective-permute-start | bytes 14155784 | tf_op jit(solution)/shard_map/ppermute | solution.py:395
  52.2 88.8 %copy-start.15 = (f32[3,2]{1,0:T(4,128)S(1)}, f32[3,2]{1,0:T(4,128)}, u32[]{:S(2)}) copy-start(f32[3,2]{1,0:T(4,128)} %multiply_tan_fusion.slopes) | copy-start | bytes 76
  52.2 153.2 %copy-start.16 = (f32[256]{0:T(256)S(1)}, f32[256]{0:T(256)}, u32[]{:S(2)}) copy-start(f32[256]{0:T(256)} %constant.95) | copy-start | bytes 3076
  68.8 60.8 %collective-permute-start.4 = (f32[48,24,128]{2,1,0:T(8,128)}, f32[48,24,128]{2,1,0:T(8,128)}, u32[]{:S(2)}, u32[]{:S(2)}) collective-permute-start(f32[48,24,128]{2,1,0:T(8,128)} %get-tuple-element.68), channel_id=1, source_target_pairs={{0,2},{2,0},{4,6},{6,4},{8,10},{10,8},{12,14},{14,12},{1,3},{3,1},... | collective-permute-start | bytes 1769480 | tf_op jit(solution)/shard_map/ppermute | solution.py:385
  70.9 68.7 %collective-permute-start.6 = (f32[48,24,128]{2,1,0:T(8,128)}, f32[48,24,128]{2,1,0:T(8,128)}, u32[]{:S(2)}, u32[]{:S(2)}) collective-permute-start(f32[48,24,128]{2,1,0:T(8,128)} %get-tuple-element.71), channel_id=1, source_target_pairs={{0,8},{2,10},{4,12},{6,14},{8,0},{10,2},{12,4},{14,6},{1,9},{3,11}... | collective-permute-start | bytes 1769480 | tf_op jit(solution)/shard_map/ppermute | solution.py:385
  73.2 79.7 %collective-permute-start.7 = (f32[48,24,128]{2,1,0:T(8,128)}, f32[48,24,128]{2,1,0:T(8,128)}, u32[]{:S(2)}, u32[]{:S(2)}) collective-permute-start(f32[48,24,128]{2,1,0:T(8,128)} %get-tuple-element.72), channel_id=1, source_target_pairs={{0,10},{2,8},{4,14},{6,12},{8,2},{10,0},{12,6},{14,4},{1,11},{3,9}... | collective-permute-start | bytes 1769480 | tf_op jit(solution)/shard_map/ppermute | solution.py:385
  126.7 119.3 %copy-start = (f32[8,16,48,128]{3,2,1,0:T(8,128)}, f32[8,16,48,128]{3,2,1,0:T(8,128)S(1)}, u32[]{:S(2)}) copy-start(f32[8,16,48,128]{3,2,1,0:T(8,128)S(1)} %all-to-all-done.head_ref) | copy-start | bytes 9437188
  126.7 62.3 %collective-permute-start.5 = (f32[48,24,128]{2,1,0:T(8,128)}, f32[48,24,128]{2,1,0:T(8,128)}, u32[]{:S(2)}, u32[]{:S(2)}) collective-permute-start(f32[48,24,128]{2,1,0:T(8,128)} %get-tuple-element.70), channel_id=1, source_target_pairs={{0,4},{2,6},{4,0},{6,2},{8,12},{10,14},{12,8},{14,10},{1,5},{3,7},... | collective-permute-start | bytes 1769480 | tf_op jit(solution)/shard_map/ppermute | solution.py:385
  126.7 75.9 %collective-permute-start.2 = (f32[48,24,128]{2,1,0:T(8,128)}, f32[48,24,128]{2,1,0:T(8,128)}, u32[]{:S(2)}, u32[]{:S(2)}) collective-permute-start(f32[48,24,128]{2,1,0:T(8,128)} %get-tuple-element.65), channel_id=1, source_target_pairs={{0,6},{2,4},{4,2},{6,0},{8,14},{10,12},{12,10},{14,8},{1,7},{3,5},... | collective-permute-start | bytes 1769480 | tf_op jit(solution)/shard_map/ppermute | solution.py:385
  129.6 73.0 %collective-permute-start.8 = (f32[48,24,128]{2,1,0:T(8,128)}, f32[48,24,128]{2,1,0:T(8,128)}, u32[]{:S(2)}, u32[]{:S(2)}) collective-permute-start(f32[48,24,128]{2,1,0:T(8,128)} %get-tuple-element.74), channel_id=1, source_target_pairs={{0,12},{2,14},{4,8},{6,10},{8,4},{10,6},{12,0},{14,2},{1,13},{3,15... | collective-permute-start | bytes 1769480 | tf_op jit(solution)/shard_map/ppermute | solution.py:385
  139.5 89.8 %collective-permute-start.9 = (f32[48,24,128]{2,1,0:T(8,128)}, f32[48,24,128]{2,1,0:T(8,128)S(1)}, u32[]{:S(2)}, u32[]{:S(2)}) collective-permute-start(f32[48,24,128]{2,1,0:T(8,128)} %get-tuple-element.76), channel_id=1, source_target_pairs={{0,14},{2,12},{4,10},{6,8},{8,6},{10,4},{12,2},{14,0},{1,15},{3,13... | collective-permute-start | bytes 1769480 | tf_op jit(solution)/shard_map/ppermute | solution.py:385
  152.9 75.0 %collective-permute-start.14 = (f32[48,16,128]{2,1,0:T(8,128)}, f32[48,16,128]{2,1,0:T(8,128)S(1)}, u32[]{:S(2)}, u32[]{:S(2)}) collective-permute-start(f32[48,16,128]{2,1,0:T(8,128)} %get-tuple-element.89), channel_id=1, source_target_pairs={{0,8},{2,10},{4,12},{6,14},{8,0},{10,2},{12,4},{14,6},{1,9},{3,11}... | collective-permute-start | bytes 1179656 | tf_op jit(solution)/shard_map/ppermute | solution.py:385
  189.0 40.3 %collective-permute-start.13 = (f32[48,16,128]{2,1,0:T(8,128)}, f32[48,16,128]{2,1,0:T(8,128)S(1)}, u32[]{:S(2)}, u32[]{:S(2)}) collective-permute-start(f32[48,16,128]{2,1,0:T(8,128)} %get-tuple-element.87), channel_id=1, source_target_pairs={{0,2},{2,0},{4,6},{6,4},{8,10},{10,8},{12,14},{14,12},{1,3},{3,1},... | collective-permute-start | bytes 1179656 | tf_op jit(solution)/shard_map/ppermute | solution.py:385
  202.6 56.7 %collective-permute-start.3 = (f32[48,16,128]{2,1,0:T(8,128)}, f32[48,16,128]{2,1,0:T(8,128)S(1)}, u32[]{:S(2)}, u32[]{:S(2)}) collective-permute-start(f32[48,16,128]{2,1,0:T(8,128)} %get-tuple-element.66), channel_id=1, source_target_pairs={{0,4},{2,6},{4,0},{6,2},{8,12},{10,14},{12,8},{14,10},{1,5},{3,7},... | collective-permute-start | bytes 1179656 | tf_op jit(solution)/shard_map/ppermute | solution.py:385
  202.6 43.5 %collective-permute-start.15 = (f32[48,16,128]{2,1,0:T(8,128)}, f32[48,16,128]{2,1,0:T(8,128)S(1)}, u32[]{:S(2)}, u32[]{:S(2)}) collective-permute-start(f32[48,16,128]{2,1,0:T(8,128)} %get-tuple-element.91), channel_id=1, source_target_pairs={{0,10},{2,8},{4,14},{6,12},{8,2},{10,0},{12,6},{14,4},{1,11},{3,9}... | collective-permute-start | bytes 1179656 | tf_op jit(solution)/shard_map/ppermute | solution.py:385
  227.9 59.1 %copy-start.3 = (f32[48,16,128]{2,1,0:T(8,128)}, f32[48,16,128]{2,1,0:T(8,128)S(1)}, u32[]{:S(2)}) copy-start(f32[48,16,128]{2,1,0:T(8,128)S(1)} %collective-permute-done.14.refs_4_) | copy-start | bytes 1179652
  227.9 31.6 %collective-permute-start.17 = (f32[48,16,128]{2,1,0:T(8,128)}, f32[48,16,128]{2,1,0:T(8,128)S(1)}, u32[]{:S(2)}, u32[]{:S(2)}) collective-permute-start(f32[48,16,128]{2,1,0:T(8,128)} %get-tuple-element.95), channel_id=1, source_target_pairs={{0,14},{2,12},{4,10},{6,8},{8,6},{10,4},{12,2},{14,0},{1,15},{3,13... | collective-permute-start | bytes 1179656 | tf_op jit(solution)/shard_map/ppermute | solution.py:385
  229.3 16.7 %copy-start.2 = (f32[48,24,128]{2,1,0:T(8,128)}, f32[48,24,128]{2,1,0:T(8,128)S(1)}, u32[]{:S(2)}) copy-start(f32[48,24,128]{2,1,0:T(8,128)S(1)} %collective-permute-done.9.refs_7_) | copy-start | bytes 1769476
  229.3 32.2 %collective-permute-start.11 = (f32[48,16,128]{2,1,0:T(8,128)}, f32[48,16,128]{2,1,0:T(8,128)S(1)}, u32[]{:S(2)}, u32[]{:S(2)}) collective-permute-start(f32[48,16,128]{2,1,0:T(8,128)} %get-tuple-element.82), channel_id=1, source_target_pairs={{0,6},{2,4},{4,2},{6,0},{8,14},{10,12},{12,10},{14,8},{1,7},{3,5},... | collective-permute-start | bytes 1179656 | tf_op jit(solution)/shard_map/ppermute | solution.py:385
  229.3 29.9 %copy-start.4 = (f32[48,16,128]{2,1,0:T(8,128)}, f32[48,16,128]{2,1,0:T(8,128)S(1)}, u32[]{:S(2)}) copy-start(f32[48,16,128]{2,1,0:T(8,128)S(1)} %collective-permute-done.13.refs_1_) | copy-start | bytes 1179652
  229.4 57.6 %collective-permute-start.16 = (f32[48,16,128]{2,1,0:T(8,128)}, f32[48,16,128]{2,1,0:T(8,128)}, u32[]{:S(2)}, u32[]{:S(2)}) collective-permute-start(f32[48,16,128]{2,1,0:T(8,128)} %get-tuple-element.93), channel_id=1, source_target_pairs={{0,12},{2,14},{4,8},{6,10},{8,4},{10,6},{12,0},{14,2},{1,13},{3,15... | collective-permute-start | bytes 1179656 | tf_op jit(solution)/shard_map/ppermute | solution.py:385
  246.0 13.2 %copy-start.6 = (f32[48,16,128]{2,1,0:T(8,128)}, f32[48,16,128]{2,1,0:T(8,128)S(1)}, u32[]{:S(2)}) copy-start(f32[48,16,128]{2,1,0:T(8,128)S(1)} %collective-permute-done.15.refs_5_) | copy-start | bytes 1179652
  246.0 37.1 %collective-permute-start.19 = (f32[48,8,128]{2,1,0:T(8,128)}, f32[48,8,128]{2,1,0:T(8,128)}, u32[]{:S(2)}, u32[]{:S(2)}) collective-permute-start(f32[48,8,128]{2,1,0:T(8,128)} %get-tuple-element.100), channel_id=1, source_target_pairs={{0,8},{2,10},{4,12},{6,14},{8,0},{10,2},{12,4},{14,6},{1,9},{3,11}... | collective-permute-start | bytes 589832 | tf_op jit(solution)/shard_map/ppermute | solution.py:385
  259.2 27.8 %copy-start.5 = (f32[48,16,128]{2,1,0:T(8,128)}, f32[48,16,128]{2,1,0:T(8,128)S(1)}, u32[]{:S(2)}) copy-start(f32[48,16,128]{2,1,0:T(8,128)S(1)} %collective-permute-done.3.refs_2_) | copy-start | bytes 1179652
  259.2 38.4 %collective-permute-start.10 = (f32[48,8,128]{2,1,0:T(8,128)}, f32[48,8,128]{2,1,0:T(8,128)S(1)}, u32[]{:S(2)}, u32[]{:S(2)}) collective-permute-start(f32[48,8,128]{2,1,0:T(8,128)} %get-tuple-element.79), channel_id=1, source_target_pairs={{0,2},{2,0},{4,6},{6,4},{8,10},{10,8},{12,14},{14,12},{1,3},{3,1},... | collective-permute-start | bytes 589832 | tf_op jit(solution)/shard_map/ppermute | solution.py:385
  259.6 27.4 %copy-start.7 = (f32[48,16,128]{2,1,0:T(8,128)}, f32[48,16,128]{2,1,0:T(8,128)S(1)}, u32[]{:S(2)}) copy-start(f32[48,16,128]{2,1,0:T(8,128)S(1)} %collective-permute-done.17.refs_7_) | copy-start | bytes 1179652
  259.6 40.2 %collective-permute-start.21 = (f32[48,8,128]{2,1,0:T(8,128)}, f32[48,8,128]{2,1,0:T(8,128)S(1)}, u32[]{:S(2)}, u32[]{:S(2)}) collective-permute-start(f32[48,8,128]{2,1,0:T(8,128)} %get-tuple-element.104), channel_id=1, source_target_pairs={{0,12},{2,14},{4,8},{6,10},{8,4},{10,6},{12,0},{14,2},{1,13},{3,15... | collective-permute-start | bytes 589832 | tf_op jit(solution)/shard_map/ppermute | solution.py:385
  261.6 25.5 %copy-start.8 = (f32[48,16,128]{2,1,0:T(8,128)}, f32[48,16,128]{2,1,0:T(8,128)S(1)}, u32[]{:S(2)}) copy-start(f32[48,16,128]{2,1,0:T(8,128)S(1)} %collective-permute-done.11.refs_3_) | copy-start | bytes 1179652
  261.6 38.3 %collective-permute-start.12 = (f32[48,8,128]{2,1,0:T(8,128)}, f32[48,8,128]{2,1,0:T(8,128)S(1)}, u32[]{:S(2)}, u32[]{:S(2)}) collective-permute-start(f32[48,8,128]{2,1,0:T(8,128)} %get-tuple-element.83), channel_id=1, source_target_pairs={{0,4},{2,6},{4,0},{6,2},{8,12},{10,14},{12,8},{14,10},{1,5},{3,7},... | collective-permute-start | bytes 589832 | tf_op jit(solution)/shard_map/ppermute | solution.py:385
  283.1 16.7 %collective-permute-start.22 = (f32[48,8,128]{2,1,0:T(8,128)}, f32[48,8,128]{2,1,0:T(8,128)S(1)}, u32[]{:S(2)}, u32[]{:S(2)}) collective-permute-start(f32[48,8,128]{2,1,0:T(8,128)} %get-tuple-element.106), channel_id=1, source_target_pairs={{0,14},{2,12},{4,10},{6,8},{8,6},{10,4},{12,2},{14,0},{1,15},{3,13... | collective-permute-start | bytes 589832 | tf_op jit(solution)/shard_map/ppermute | solution.py:385
  287.0 17.2 %collective-permute-start.20 = (f32[48,8,128]{2,1,0:T(8,128)}, f32[48,8,128]{2,1,0:T(8,128)S(1)}, u32[]{:S(2)}, u32[]{:S(2)}) collective-permute-start(f32[48,8,128]{2,1,0:T(8,128)} %get-tuple-element.102), channel_id=1, source_target_pairs={{0,10},{2,8},{4,14},{6,12},{8,2},{10,0},{12,6},{14,4},{1,11},{3,9}... | collective-permute-start | bytes 589832 | tf_op jit(solution)/shard_map/ppermute | solution.py:385
  287.0 10.7 %copy-start.17 = (f32[48,8,128]{2,1,0:T(8,128)S(1)}, f32[48,8,128]{2,1,0:T(8,128)}, u32[]{:S(2)}) copy-start(f32[48,8,128]{2,1,0:T(8,128)} %get-tuple-element.98) | copy-start | bytes 589828
  297.7 10.7 %copy-start.9 = (f32[48,8,128]{2,1,0:T(8,128)}, f32[48,8,128]{2,1,0:T(8,128)S(1)}, u32[]{:S(2)}) copy-start(f32[48,8,128]{2,1,0:T(8,128)S(1)} %collective-permute-done.10.refs_1_) | copy-start | bytes 589828
  297.7 10.6 %collective-permute-start.18 = (f32[48,8,128]{2,1,0:T(8,128)S(1)}, f32[48,8,128]{2,1,0:T(8,128)S(1)}, u32[]{:S(2)}, u32[]{:S(2)}) collective-permute-start(f32[48,8,128]{2,1,0:T(8,128)S(1)} %copy-done.17), channel_id=1, source_target_pairs={{0,6},{2,4},{4,2},{6,0},{8,14},{10,12},{12,10},{14,8},{1,7},{3,5},... | collective-permute-start | bytes 589832 | tf_op jit(solution)/shard_map/ppermute | solution.py:385
  299.8 8.5 %copy-start.10 = (f32[48,8,128]{2,1,0:T(8,128)}, f32[48,8,128]{2,1,0:T(8,128)S(1)}, u32[]{:S(2)}) copy-start(f32[48,8,128]{2,1,0:T(8,128)S(1)} %collective-permute-done.21.refs_6_) | copy-start | bytes 589828
  299.8 8.5 %copy-start.11 = (f32[48,8,128]{2,1,0:T(8,128)}, f32[48,8,128]{2,1,0:T(8,128)S(1)}, u32[]{:S(2)}) copy-start(f32[48,8,128]{2,1,0:T(8,128)S(1)} %collective-permute-done.12.refs_2_) | copy-start | bytes 589828
  299.9 8.5 %copy-start.12 = (f32[48,8,128]{2,1,0:T(8,128)}, f32[48,8,128]{2,1,0:T(8,128)S(1)}, u32[]{:S(2)}) copy-start(f32[48,8,128]{2,1,0:T(8,128)S(1)} %collective-permute-done.22.refs_7_) | copy-start | bytes 589828
  304.2 4.1 %copy-start.13 = (f32[48,8,128]{2,1,0:T(8,128)}, f32[48,8,128]{2,1,0:T(8,128)S(1)}, u32[]{:S(2)}) copy-start(f32[48,8,128]{2,1,0:T(8,128)S(1)} %collective-permute-done.20.refs_5_) | copy-start | bytes 589828
  308.3 0.7 copy-start.14

commit v4 on v2

--- a/solution.py
+++ b/solution.py
@@ -17,7 +17,7 @@
 XB = 8
 HEAD = 2
 CHUNKS = (3, 2, 1)
-GATES = (2,)
+GATES = (3,)
 WINDOW = 5
 
 

time: 313 us -> 313 us (level)
  waiting for transfers between devices: 185 us -> 145 us
  starting transfers between devices: 39.4 us -> 77.8 us
    ppermute x21, starting transfers between devices: 31.7 us -> 70.2 us  [spread(): lax.ppermute(after(pieces[d], *others), 'row', [(i, i ^ d) for i in range...]
    ppermute x21, waiting for transfers between devices: 120 us -> 93.9 us  [spread(): lax.ppermute(after(pieces[d], *others), 'row', [(i, i ^ d) for i in range...]
    all_to_all x1, waiting for transfers between devices: 53.4 us -> 39.3 us  [body(): head = lax.all_to_all(head, 'row', 0, 0, tiled=True)]
  transfers between devices with their start and end apart: 24 -> 24, of which waited for: 11 -> 9; matrix products, arithmetic and copies ran while one was open for 2% -> 2% of each run, Pallas kernels for 18% -> 18%
where the time goes in v4:
time: 313 us; the launch traced here: 311 us
  waiting for transfers between devices  145 us (46%)
  starting transfers between devices  77.8 us (25%)
  Pallas kernels  77.4 us (25%)
  other arithmetic  7.64 us (2%)
  local copies, waits for them, and re-layouts  3.22 us (1%)
    ppermute x21, waiting for transfers between devices, spread(): lax.ppermute(after(pieces[d], *others), 'row', [(i, i ^ d) for i in range...  93.9 us
    ppermute x21, starting transfers between devices, spread(): lax.ppermute(after(pieces[d], *others), 'row', [(i, i ^ d) for i in range...  70.2 us
    all_to_all x1, waiting for transfers between devices, body(): head = lax.all_to_all(head, 'row', 0, 0, tiled=True)  39.3 us
    pallas_call x3, Pallas kernels, first(): call(first_kernel, height // rows, specs, [pl.BlockSpec((nx, rows, nk), l...  30.9 us
    pallas_call x2, Pallas kernels, second(): call(functools.partial(second_kernel, x0, heights, part, full), size // x...  24.8 us
    pallas_call x2, Pallas kernels, third(): call(functools.partial(third_kernel, x0, size, full), size // xb, [pl.Blo...  21.7 us
    ppermute x1, waiting for transfers between devices, body(): lax.ppermute(other, 'col', swap)  8.25 us
    all_to_all x1, starting transfers between devices, body(): head = lax.all_to_all(head, 'row', 0, 0, tiled=True)  7.2 us
  transfers between devices with their start and end apart: 24, of which 9 were waited for; matrix products, arithmetic and copies ran while one was open for 2% of the time, Pallas kernels for 18%

profile of v4, /device:TPU:0, one launch (start us, length us, event | category | flops | bytes accessed | tf_op | source)
XLA Modules:
  0.0 311.0 jit_solution(5415356777112713930)
XLA Ops:
  0.0 0.8 copy.17
  0.8 0.6 multiply_tan_fusion.slopes
  1.4 0.6 pad_add_fusion.place
  2.0 7.2 %third.2 = (f32[16,192,128]{2,1,0:T(8,128)}, f32[16,192,128]{2,1,0:T(8,128)}) custom-call(s32[4]{0:T(128)} %pad_add_fusion.place, f32[3,2]{1,0:T(4,128)} %multiply_tan_fusion.slopes, f32[64,192,256]{2,1,0:T(8,128)} %v_ref.2, bf16[768,256]{1,0:T(8,128)(2,1)} %constant.82.clone.fw_ref, bf16[768,256]{1,0:T(8,128)(2,1)} %constant.83.clone.iv_ref), custom_call_target="tpu_custom_call" | custom-call | flops 1 | bytes 1 | tf_op jit(solution)/shard_map/third/pallas_call | solution.py:347
  9.1 0.5 collective-permute-start
  9.6 3.2 %collective-permute-done.other_ref = f32[16,192,128]{2,1,0:T(8,128)S(1)} collective-permute-done((f32[16,192,128]{2,1,0:T(8,128)}, f32[16,192,128]{2,1,0:T(8,128)S(1)}, u32[]{:S(2)}, u32[]{:S(2)}) %collective-permute-start) | collective-permute-done | bytes 1572896 | tf_op jit(solution)/shard_map/ppermute | solution.py:391
  12.8 1.2 copy-done.1
  14.0 8.1 %second.2 = f32[8,16,48,128]{3,2,1,0:T(8,128)} custom-call(s32[4]{0:T(128)} %pad_add_fusion.place, f32[3,2]{1,0:T(4,128)} %multiply_tan_fusion.slopes, f32[16,192,128]{2,1,0:T(8,128)} %get-tuple-element.57.own_ref, f32[16,192,128]{2,1,0:T(8,128)} %copy-done.1, bf16[192,576]{1,0:T(8,128)(2,1)} %constant.84.clone.fe_ref, ...), custom_call_target="tpu_custom_call" | custom-call | flops 1 | bytes 1 | tf_op jit(solution)/shard_map/second/pallas_call | solution.py:367
  22.1 7.2 %all-to-all-start = ((f32[8,16,48,128]{3,2,1,0:T(8,128)}), f32[8,16,48,128]{3,2,1,0:T(8,128)S(1)}, u32[]{:S(2)}, u32[]{:S(2)}) async-start(f32[8,16,48,128]{3,2,1,0:T(8,128)} %second.2), calls=%async_computation | async-start | bytes 6291456 | tf_op jit(solution)/shard_map/all_to_all | solution.py:393
  29.3 14.6 %third.3 = (f32[48,192,128]{2,1,0:T(8,128)}, f32[48,192,128]{2,1,0:T(8,128)}) custom-call(s32[4]{0:T(128)} %pad_add_fusion.place, f32[3,2]{1,0:T(4,128)} %multiply_tan_fusion.slopes, f32[64,192,256]{2,1,0:T(8,128)} %v_ref.2, bf16[768,256]{1,0:T(8,128)(2,1)} %constant.82.clone.fw_ref, bf16[768,256]{1,0:T(8,128)(2,1)} %constant.83.clone.iv_ref), custom_call_target="tpu_custom_call" | custom-call | flops 1 | bytes 1 | tf_op jit(solution)/shard_map/third/pallas_call | solution.py:347
  43.9 0.0 collective-permute-start.1
  43.9 8.2 %collective-permute-done.1.other_ref = f32[48,192,128]{2,1,0:T(8,128)} collective-permute-done((f32[48,192,128]{2,1,0:T(8,128)}, f32[48,192,128]{2,1,0:T(8,128)}, u32[]{:S(2)}, u32[]{:S(2)}) %collective-permute-start.1) | collective-permute-done | bytes 4718624 | tf_op jit(solution)/shard_map/ppermute | solution.py:395
  52.2 16.6 %second.3 = (f32[48,24,128]{2,1,0:T(8,128)}, f32[48,16,128]{2,1,0:T(8,128)}, f32[48,8,128]{2,1,0:T(8,128)}, f32[48,24,128]{2,1,0:T(8,128)}, f32[48,16,128]{2,1,0...) custom-call(s32[4]{0:T(128)} %pad_add_fusion.place, ...), custom_call_target="tpu_custom_call" | custom-call | flops 1 | bytes 1 | tf_op jit(solution)/shard_map/second/pallas_call | solution.py:367
  68.8 2.1 collective-permute-start.4
  70.9 2.4 collective-permute-start.6
  73.3 1.5 collective-permute-start.5
  74.7 39.3 %all-to-all-done.head_ref = f32[8,16,48,128]{3,2,1,0:T(8,128)S(1)} async-done(((f32[8,16,48,128]{3,2,1,0:T(8,128)}), f32[8,16,48,128]{3,2,1,0:T(8,128)S(1)}, u32[]{:S(2)}, u32[]{:S(2)}) %all-to-all-start) | async-done | bytes 3145760 | tf_op jit(solution)/shard_map/all_to_all | solution.py:393
  114.1 0.5 collective-permute-start.7
  114.5 2.3 collective-permute-start.2
  116.8 0.0 collective-permute-done.4.refs_1_
  116.8 2.5 collective-permute-start.8
  119.3 20.2 %collective-permute-done.6.refs_4_ = f32[48,24,128]{2,1,0:T(8,128)} collective-permute-done((f32[48,24,128]{2,1,0:T(8,128)}, f32[48,24,128]{2,1,0:T(8,128)}, u32[]{:S(2)}, u32[]{:S(2)}) %collective-permute-start.6) | collective-permute-done | bytes 589856 | tf_op jit(solution)/shard_map/ppermute | solution.py:385
  139.5 1.3 collective-permute-start.9
  140.8 0.6 fusion.4
  141.4 1.4 collective-permute-start.18
  142.8 35.4 %collective-permute-done.7.refs_5_ = f32[48,24,128]{2,1,0:T(8,128)} collective-permute-done((f32[48,24,128]{2,1,0:T(8,128)}, f32[48,24,128]{2,1,0:T(8,128)}, u32[]{:S(2)}, u32[]{:S(2)}) %collective-permute-start.7) | collective-permute-done | bytes 589856 | tf_op jit(solution)/shard_map/ppermute | solution.py:385
  178.2 0.7 add_multiply_fusion
  178.9 1.1 collective-permute-start.3
  180.1 0.0 collective-permute-done.8.refs_6_
  180.1 18.8 %collective-permute-start.16 = (f32[48,16,128]{2,1,0:T(8,128)}, f32[48,16,128]{2,1,0:T(8,128)S(1)}, u32[]{:S(2)}, u32[]{:S(2)}) collective-permute-start(f32[48,16,128]{2,1,0:T(8,128)} %get-tuple-element.92), channel_id=1, source_target_pairs={{0,10},{2,8},{4,14},{6,12},{8,2},{10,0},{12,6},{14,4},{1,11},{3,9}... | collective-permute-start | bytes 1179656 | tf_op jit(solution)/shard_map/ppermute | solution.py:385
  198.9 3.9 %fusion = (f32[6,256,8]{2,1,0:T(8,128)}, f32[6,256,8]{2,1,0:T(8,128)}) fusion(f32[6,8]{1,0:T(8,128)S(1)} %add_multiply_fusion, f32[256]{0:T(256)S(1)} %copy-done.16), kind=kLoop, calls=%fused_computation.1 | loop fusion | flops 24576 | bytes 99520 | tf_op jit(solution)/shard_map/sin | solution.py:400
  202.8 0.7 add_multiply_fusion.1
  203.5 3.4 %collective-permute-start.19 = (f32[48,16,128]{2,1,0:T(8,128)}, f32[48,16,128]{2,1,0:T(8,128)S(1)}, u32[]{:S(2)}, u32[]{:S(2)}) collective-permute-start(f32[48,16,128]{2,1,0:T(8,128)} %get-tuple-element.98), channel_id=1, source_target_pairs={{0,12},{2,14},{4,8},{6,10},{8,4},{10,6},{12,0},{14,2},{1,13},{3,15... | collective-permute-start | bytes 1179656 | tf_op jit(solution)/shard_map/ppermute | solution.py:385
  206.8 22.5 %collective-permute-start.11 = (f32[48,16,128]{2,1,0:T(8,128)}, f32[48,16,128]{2,1,0:T(8,128)S(1)}, u32[]{:S(2)}, u32[]{:S(2)}) collective-permute-start(f32[48,16,128]{2,1,0:T(8,128)} %get-tuple-element.82), channel_id=1, source_target_pairs={{0,6},{2,4},{4,2},{6,0},{8,14},{10,12},{12,10},{14,8},{1,7},{3,5},... | collective-permute-start | bytes 1179656 | tf_op jit(solution)/shard_map/ppermute | solution.py:385
  229.3 7.1 %collective-permute-done.13.refs_4_ = f32[48,16,128]{2,1,0:T(8,128)S(1)} collective-permute-done((f32[48,16,128]{2,1,0:T(8,128)}, f32[48,16,128]{2,1,0:T(8,128)S(1)}, u32[]{:S(2)}, u32[]{:S(2)}) %collective-permute-start.13) | collective-permute-done | bytes 393248 | tf_op jit(solution)/shard_map/ppermute | solution.py:385
  236.4 1.3 collective-permute-start.14
  237.7 1.3 fusion.2
  239.0 15.0 %collective-permute-done.16.refs_5_ = f32[48,16,128]{2,1,0:T(8,128)S(1)} collective-permute-done((f32[48,16,128]{2,1,0:T(8,128)}, f32[48,16,128]{2,1,0:T(8,128)S(1)}, u32[]{:S(2)}, u32[]{:S(2)}) %collective-permute-start.16) | collective-permute-done | bytes 393248 | tf_op jit(solution)/shard_map/ppermute | solution.py:385
  254.0 13.2 %first.3 = (f32[512,48,128]{2,1,0:T(8,128)}, f32[8,128]{1,0:T(8,128)}) custom-call(s32[4]{0:T(128)} %pad_add_fusion.place, f32[3,2]{1,0:T(4,128)} %multiply_tan_fusion.slopes, f32[8,16,48,128]{3,2,1,0:T(8,128)} %copy-done, f32[48,24,128]{2,1,0:T(8,128)} %get-tuple-element.67.refs_0_, f32[48,24,128]{2,1,0:T(8,128)} %collective-permute-done.4.refs_1_, ...), custom_call_target="tpu_custom_call" | custom-call | flops 1 | bytes 1 | tf_op jit(solution)/shard_map/first/pallas_call | solution.py:424
  267.2 0.7 collective-permute-start.10
  267.9 3.7 %collective-permute-start.20 = (f32[48,8,128]{2,1,0:T(8,128)}, f32[48,8,128]{2,1,0:T(8,128)S(1)}, u32[]{:S(2)}, u32[]{:S(2)}) collective-permute-start(f32[48,8,128]{2,1,0:T(8,128)} %get-tuple-element.99), channel_id=1, source_target_pairs={{0,10},{2,8},{4,14},{6,12},{8,2},{10,0},{12,6},{14,4},{1,11},{3,9}... | collective-permute-start | bytes 589832 | tf_op jit(solution)/shard_map/ppermute | solution.py:385
  271.7 11.1 %collective-permute-done.17.refs_4_ = f32[48,8,128]{2,1,0:T(8,128)} collective-permute-done((f32[48,8,128]{2,1,0:T(8,128)}, f32[48,8,128]{2,1,0:T(8,128)}, u32[]{:S(2)}, u32[]{:S(2)}) %collective-permute-start.17) | collective-permute-done | bytes 196640 | tf_op jit(solution)/shard_map/ppermute | solution.py:385
  282.8 1.3 collective-permute-start.22
  284.2 10.6 %first.4 = (f32[512,48,128]{2,1,0:T(8,128)}, f32[8,128]{1,0:T(8,128)}) custom-call(s32[4]{0:T(128)} %pad_add_fusion.place, f32[3,2]{1,0:T(4,128)} %multiply_tan_fusion.slopes, f32[8,16,48,128]{3,2,1,0:T(8,128)} %copy-done, f32[48,16,128]{2,1,0:T(8,128)} %get-tuple-element.101.refs_0_, f32[48,16,128]{2,1,0:T(8,128)} %copy-done.3, ...), custom_call_target="tpu_custom_call", output_to_operand_aliasing={{0}: (19, {})} | custom-call | flops 1 | bytes 1 | tf_op jit(solution)/shard_map/first/pallas_call | solution.py:424
  294.9 3.4 %collective-permute-start.21 = (f32[48,8,128]{2,1,0:T(8,128)S(1)}, f32[48,8,128]{2,1,0:T(8,128)S(1)}, u32[]{:S(2)}, u32[]{:S(2)}) collective-permute-start(f32[48,8,128]{2,1,0:T(8,128)S(1)} %copy-done.17), channel_id=1, source_target_pairs={{0,12},{2,14},{4,8},{6,10},{8,4},{10,6},{12,0},{14,2},{1,13},{3,15... | collective-permute-start | bytes 589832 | tf_op jit(solution)/shard_map/ppermute | solution.py:385
  298.3 5.0 %collective-permute-done.21.refs_6_ = f32[48,8,128]{2,1,0:T(8,128)S(1)} collective-permute-done((f32[48,8,128]{2,1,0:T(8,128)S(1)}, f32[48,8,128]{2,1,0:T(8,128)S(1)}, u32[]{:S(2)}, u32[]{:S(2)}) %collective-permute-start.21) | collective-permute-done | bytes 196640 | tf_op jit(solution)/shard_map/ppermute | solution.py:385
  303.3 0.6 copy-done.14
  303.9 7.1 %first.5 = (f32[512,48,128]{2,1,0:T(8,128)}, f32[8,128]{1,0:T(8,128)}) custom-call(s32[4]{0:T(128)} %pad_add_fusion.place, f32[3,2]{1,0:T(4,128)} %multiply_tan_fusion.slopes, f32[8,16,48,128]{3,2,1,0:T(8,128)} %copy-done, f32[48,8,128]{2,1,0:T(8,128)} %get-tuple-element.62.refs_0_, f32[48,8,128]{2,1,0:T(8,128)} %copy-done.9, ...), custom_call_target="tpu_custom_call", output_to_operand_aliasing={{0}: (19, {})} | custom-call | flops 1 | bytes 1 | tf_op jit(solution)/shard_map/first/pallas_call | solution.py:424
  (51 shorter events, 0.1 us)
Async XLA Ops:
  9.1 3.7 %collective-permute-start = (f32[16,192,128]{2,1,0:T(8,128)}, f32[16,192,128]{2,1,0:T(8,128)S(1)}, u32[]{:S(2)}, u32[]{:S(2)}) collective-permute-start(f32[16,192,128]{2,1,0:T(8,128)} %get-tuple-element.58), channel_id=1, source_target_pairs={{0,1},{1,0},{2,3},{3,2},{4,5},{5,4},{6,7},{7,6},{8,9},{9,8},{10,11... | collective-permute-start | bytes 4718600 | tf_op jit(solution)/shard_map/ppermute | solution.py:391
  12.8 1.2 copy-start.1
  22.1 91.9 %all-to-all-start = ((f32[8,16,48,128]{3,2,1,0:T(8,128)}), f32[8,16,48,128]{3,2,1,0:T(8,128)S(1)}, u32[]{:S(2)}, u32[]{:S(2)}) async-start(f32[8,16,48,128]{3,2,1,0:T(8,128)} %second.2), calls=%async_computation | async-start | bytes 6291456 | tf_op jit(solution)/shard_map/all_to_all | solution.py:393
  43.9 8.3 %collective-permute-start.1 = (f32[48,192,128]{2,1,0:T(8,128)}, f32[48,192,128]{2,1,0:T(8,128)}, u32[]{:S(2)}, u32[]{:S(2)}) collective-permute-start(f32[48,192,128]{2,1,0:T(8,128)} %get-tuple-element.61), channel_id=1, source_target_pairs={{0,1},{1,0},{2,3},{3,2},{4,5},{5,4},{6,7},{7,6},{8,9},{9,8},{10,11... | collective-permute-start | bytes 14155784 | tf_op jit(solution)/shard_map/ppermute | solution.py:395
  52.2 88.7 %copy-start.15 = (f32[3,2]{1,0:T(4,128)S(1)}, f32[3,2]{1,0:T(4,128)}, u32[]{:S(2)}) copy-start(f32[3,2]{1,0:T(4,128)} %multiply_tan_fusion.slopes) | copy-start | bytes 76
  52.2 146.7 %copy-start.16 = (f32[256]{0:T(256)S(1)}, f32[256]{0:T(256)}, u32[]{:S(2)}) copy-start(f32[256]{0:T(256)} %constant.95) | copy-start | bytes 3076
  68.8 48.0 %collective-permute-start.4 = (f32[48,24,128]{2,1,0:T(8,128)}, f32[48,24,128]{2,1,0:T(8,128)}, u32[]{:S(2)}, u32[]{:S(2)}) collective-permute-start(f32[48,24,128]{2,1,0:T(8,128)} %get-tuple-element.68), channel_id=1, source_target_pairs={{0,2},{2,0},{4,6},{6,4},{8,10},{10,8},{12,14},{14,12},{1,3},{3,1},... | collective-permute-start | bytes 1769480 | tf_op jit(solution)/shard_map/ppermute | solution.py:385
  70.9 68.6 %collective-permute-start.6 = (f32[48,24,128]{2,1,0:T(8,128)}, f32[48,24,128]{2,1,0:T(8,128)}, u32[]{:S(2)}, u32[]{:S(2)}) collective-permute-start(f32[48,24,128]{2,1,0:T(8,128)} %get-tuple-element.70), channel_id=1, source_target_pairs={{0,8},{2,10},{4,12},{6,14},{8,0},{10,2},{12,4},{14,6},{1,9},{3,11}... | collective-permute-start | bytes 1769480 | tf_op jit(solution)/shard_map/ppermute | solution.py:385
  73.3 68.1 %collective-permute-start.5 = (f32[48,24,128]{2,1,0:T(8,128)}, f32[48,24,128]{2,1,0:T(8,128)}, u32[]{:S(2)}, u32[]{:S(2)}) collective-permute-start(f32[48,24,128]{2,1,0:T(8,128)} %get-tuple-element.69), channel_id=1, source_target_pairs={{0,4},{2,6},{4,0},{6,2},{8,12},{10,14},{12,8},{14,10},{1,5},{3,7},... | collective-permute-start | bytes 1769480 | tf_op jit(solution)/shard_map/ppermute | solution.py:385
  114.0 140.0 %copy-start = (f32[8,16,48,128]{3,2,1,0:T(8,128)}, f32[8,16,48,128]{3,2,1,0:T(8,128)S(1)}, u32[]{:S(2)}) copy-start(f32[8,16,48,128]{3,2,1,0:T(8,128)S(1)} %all-to-all-done.head_ref) | copy-start | bytes 9437188
  114.1 64.2 %collective-permute-start.7 = (f32[48,24,128]{2,1,0:T(8,128)}, f32[48,24,128]{2,1,0:T(8,128)}, u32[]{:S(2)}, u32[]{:S(2)}) collective-permute-start(f32[48,24,128]{2,1,0:T(8,128)} %get-tuple-element.72), channel_id=1, source_target_pairs={{0,10},{2,8},{4,14},{6,12},{8,2},{10,0},{12,6},{14,4},{1,11},{3,9}... | collective-permute-start | bytes 1769480 | tf_op jit(solution)/shard_map/ppermute | solution.py:385
  114.5 64.4 %collective-permute-start.2 = (f32[48,24,128]{2,1,0:T(8,128)}, f32[48,24,128]{2,1,0:T(8,128)}, u32[]{:S(2)}, u32[]{:S(2)}) collective-permute-start(f32[48,24,128]{2,1,0:T(8,128)} %get-tuple-element.65), channel_id=1, source_target_pairs={{0,6},{2,4},{4,2},{6,0},{8,14},{10,12},{12,10},{14,8},{1,7},{3,5},... | collective-permute-start | bytes 1769480 | tf_op jit(solution)/shard_map/ppermute | solution.py:385
  116.8 63.3 %collective-permute-start.8 = (f32[48,24,128]{2,1,0:T(8,128)}, f32[48,24,128]{2,1,0:T(8,128)}, u32[]{:S(2)}, u32[]{:S(2)}) collective-permute-start(f32[48,24,128]{2,1,0:T(8,128)} %get-tuple-element.74), channel_id=1, source_target_pairs={{0,12},{2,14},{4,8},{6,10},{8,4},{10,6},{12,0},{14,2},{1,13},{3,15... | collective-permute-start | bytes 1769480 | tf_op jit(solution)/shard_map/ppermute | solution.py:385
  139.5 67.3 %collective-permute-start.9 = (f32[48,24,128]{2,1,0:T(8,128)}, f32[48,24,128]{2,1,0:T(8,128)S(1)}, u32[]{:S(2)}, u32[]{:S(2)}) collective-permute-start(f32[48,24,128]{2,1,0:T(8,128)} %get-tuple-element.76), channel_id=1, source_target_pairs={{0,14},{2,12},{4,10},{6,8},{8,6},{10,4},{12,2},{14,0},{1,15},{3,13... | collective-permute-start | bytes 1769480 | tf_op jit(solution)/shard_map/ppermute | solution.py:385
  141.4 62.0 %collective-permute-start.18 = (f32[48,16,128]{2,1,0:T(8,128)}, f32[48,16,128]{2,1,0:T(8,128)S(1)}, u32[]{:S(2)}, u32[]{:S(2)}) collective-permute-start(f32[48,16,128]{2,1,0:T(8,128)} %get-tuple-element.97), channel_id=1, source_target_pairs={{0,2},{2,0},{4,6},{6,4},{8,10},{10,8},{12,14},{14,12},{1,3},{3,1},... | collective-permute-start | bytes 1179656 | tf_op jit(solution)/shard_map/ppermute | solution.py:385
  178.2 58.1 %collective-permute-start.13 = (f32[48,16,128]{2,1,0:T(8,128)}, f32[48,16,128]{2,1,0:T(8,128)S(1)}, u32[]{:S(2)}, u32[]{:S(2)}) collective-permute-start(f32[48,16,128]{2,1,0:T(8,128)} %get-tuple-element.87), channel_id=1, source_target_pairs={{0,8},{2,10},{4,12},{6,14},{8,0},{10,2},{12,4},{14,6},{1,9},{3,11}... | collective-permute-start | bytes 1179656 | tf_op jit(solution)/shard_map/ppermute | solution.py:385
  178.9 88.3 %collective-permute-start.3 = (f32[48,16,128]{2,1,0:T(8,128)}, f32[48,16,128]{2,1,0:T(8,128)S(1)}, u32[]{:S(2)}, u32[]{:S(2)}) collective-permute-start(f32[48,16,128]{2,1,0:T(8,128)} %get-tuple-element.66), channel_id=1, source_target_pairs={{0,4},{2,6},{4,0},{6,2},{8,12},{10,14},{12,8},{14,10},{1,5},{3,7},... | collective-permute-start | bytes 1179656 | tf_op jit(solution)/shard_map/ppermute | solution.py:385
  180.1 73.9 %collective-permute-start.16 = (f32[48,16,128]{2,1,0:T(8,128)}, f32[48,16,128]{2,1,0:T(8,128)S(1)}, u32[]{:S(2)}, u32[]{:S(2)}) collective-permute-start(f32[48,16,128]{2,1,0:T(8,128)} %get-tuple-element.92), channel_id=1, source_target_pairs={{0,10},{2,8},{4,14},{6,12},{8,2},{10,0},{12,6},{14,4},{1,11},{3,9}... | collective-permute-start | bytes 1179656 | tf_op jit(solution)/shard_map/ppermute | solution.py:385
  203.4 80.7 %copy-start.3 = (f32[48,16,128]{2,1,0:T(8,128)}, f32[48,16,128]{2,1,0:T(8,128)S(1)}, u32[]{:S(2)}) copy-start(f32[48,16,128]{2,1,0:T(8,128)S(1)} %collective-permute-done.18.refs_1_) | copy-start | bytes 1179652
  203.5 64.5 %collective-permute-start.19 = (f32[48,16,128]{2,1,0:T(8,128)}, f32[48,16,128]{2,1,0:T(8,128)S(1)}, u32[]{:S(2)}, u32[]{:S(2)}) collective-permute-start(f32[48,16,128]{2,1,0:T(8,128)} %get-tuple-element.98), channel_id=1, source_target_pairs={{0,12},{2,14},{4,8},{6,10},{8,4},{10,6},{12,0},{14,2},{1,13},{3,15... | collective-permute-start | bytes 1179656 | tf_op jit(solution)/shard_map/ppermute | solution.py:385
  206.8 47.2 %copy-start.2 = (f32[48,24,128]{2,1,0:T(8,128)}, f32[48,24,128]{2,1,0:T(8,128)S(1)}, u32[]{:S(2)}) copy-start(f32[48,24,128]{2,1,0:T(8,128)S(1)} %collective-permute-done.9.refs_7_) | copy-start | bytes 1769476
  206.8 64.8 %collective-permute-start.11 = (f32[48,16,128]{2,1,0:T(8,128)}, f32[48,16,128]{2,1,0:T(8,128)S(1)}, u32[]{:S(2)}, u32[]{:S(2)}) collective-permute-start(f32[48,16,128]{2,1,0:T(8,128)} %get-tuple-element.82), channel_id=1, source_target_pairs={{0,6},{2,4},{4,2},{6,0},{8,14},{10,12},{12,10},{14,8},{1,7},{3,5},... | collective-permute-start | bytes 1179656 | tf_op jit(solution)/shard_map/ppermute | solution.py:385
  236.4 30.8 %copy-start.4 = (f32[48,16,128]{2,1,0:T(8,128)}, f32[48,16,128]{2,1,0:T(8,128)S(1)}, u32[]{:S(2)}) copy-start(f32[48,16,128]{2,1,0:T(8,128)S(1)} %collective-permute-done.13.refs_4_) | copy-start | bytes 1179652
  236.4 47.8 %collective-permute-start.14 = (f32[48,16,128]{2,1,0:T(8,128)}, f32[48,16,128]{2,1,0:T(8,128)}, u32[]{:S(2)}, u32[]{:S(2)}) collective-permute-start(f32[48,16,128]{2,1,0:T(8,128)} %get-tuple-element.88), channel_id=1, source_target_pairs={{0,14},{2,12},{4,10},{6,8},{8,6},{10,4},{12,2},{14,0},{1,15},{3,13... | collective-permute-start | bytes 1179656 | tf_op jit(solution)/shard_map/ppermute | solution.py:385
  254.0 13.2 %copy-start.6 = (f32[48,16,128]{2,1,0:T(8,128)}, f32[48,16,128]{2,1,0:T(8,128)S(1)}, u32[]{:S(2)}) copy-start(f32[48,16,128]{2,1,0:T(8,128)S(1)} %collective-permute-done.16.refs_5_) | copy-start | bytes 1179652
  254.0 28.8 %collective-permute-start.17 = (f32[48,8,128]{2,1,0:T(8,128)}, f32[48,8,128]{2,1,0:T(8,128)}, u32[]{:S(2)}, u32[]{:S(2)}) collective-permute-start(f32[48,8,128]{2,1,0:T(8,128)} %get-tuple-element.93), channel_id=1, source_target_pairs={{0,8},{2,10},{4,12},{6,14},{8,0},{10,2},{12,4},{14,6},{1,9},{3,11}... | collective-permute-start | bytes 589832 | tf_op jit(solution)/shard_map/ppermute | solution.py:385
  267.2 16.9 %copy-start.5 = (f32[48,16,128]{2,1,0:T(8,128)}, f32[48,16,128]{2,1,0:T(8,128)S(1)}, u32[]{:S(2)}) copy-start(f32[48,16,128]{2,1,0:T(8,128)S(1)} %collective-permute-done.3.refs_2_) | copy-start | bytes 1179652
  267.2 27.6 %collective-permute-start.10 = (f32[48,8,128]{2,1,0:T(8,128)}, f32[48,8,128]{2,1,0:T(8,128)S(1)}, u32[]{:S(2)}, u32[]{:S(2)}) collective-permute-start(f32[48,8,128]{2,1,0:T(8,128)} %get-tuple-element.79), channel_id=1, source_target_pairs={{0,2},{2,0},{4,6},{6,4},{8,10},{10,8},{12,14},{14,12},{1,3},{3,1},... | collective-permute-start | bytes 589832 | tf_op jit(solution)/shard_map/ppermute | solution.py:385
  267.9 16.2 %copy-start.7 = (f32[48,16,128]{2,1,0:T(8,128)}, f32[48,16,128]{2,1,0:T(8,128)S(1)}, u32[]{:S(2)}) copy-start(f32[48,16,128]{2,1,0:T(8,128)S(1)} %collective-permute-done.19.refs_6_) | copy-start | bytes 1179652
  267.9 30.3 %collective-permute-start.20 = (f32[48,8,128]{2,1,0:T(8,128)}, f32[48,8,128]{2,1,0:T(8,128)S(1)}, u32[]{:S(2)}, u32[]{:S(2)}) collective-permute-start(f32[48,8,128]{2,1,0:T(8,128)} %get-tuple-element.99), channel_id=1, source_target_pairs={{0,10},{2,8},{4,14},{6,12},{8,2},{10,0},{12,6},{14,4},{1,11},{3,9}... | collective-permute-start | bytes 589832 | tf_op jit(solution)/shard_map/ppermute | solution.py:385
  271.7 12.5 %copy-start.8 = (f32[48,16,128]{2,1,0:T(8,128)}, f32[48,16,128]{2,1,0:T(8,128)S(1)}, u32[]{:S(2)}) copy-start(f32[48,16,128]{2,1,0:T(8,128)S(1)} %collective-permute-done.11.refs_3_) | copy-start | bytes 1179652
  271.7 26.6 %collective-permute-start.12 = (f32[48,8,128]{2,1,0:T(8,128)}, f32[48,8,128]{2,1,0:T(8,128)S(1)}, u32[]{:S(2)}, u32[]{:S(2)}) collective-permute-start(f32[48,8,128]{2,1,0:T(8,128)} %get-tuple-element.83), channel_id=1, source_target_pairs={{0,4},{2,6},{4,0},{6,2},{8,12},{10,14},{12,8},{14,10},{1,5},{3,7},... | collective-permute-start | bytes 589832 | tf_op jit(solution)/shard_map/ppermute | solution.py:385
  282.8 15.5 %collective-permute-start.22 = (f32[48,8,128]{2,1,0:T(8,128)}, f32[48,8,128]{2,1,0:T(8,128)S(1)}, u32[]{:S(2)}, u32[]{:S(2)}) collective-permute-start(f32[48,8,128]{2,1,0:T(8,128)} %get-tuple-element.106), channel_id=1, source_target_pairs={{0,14},{2,12},{4,10},{6,8},{8,6},{10,4},{12,2},{14,0},{1,15},{3,13... | collective-permute-start | bytes 589832 | tf_op jit(solution)/shard_map/ppermute | solution.py:385
  284.2 14.1 %collective-permute-start.15 = (f32[48,8,128]{2,1,0:T(8,128)}, f32[48,8,128]{2,1,0:T(8,128)S(1)}, u32[]{:S(2)}, u32[]{:S(2)}) collective-permute-start(f32[48,8,128]{2,1,0:T(8,128)} %get-tuple-element.89), channel_id=1, source_target_pairs={{0,6},{2,4},{4,2},{6,0},{8,14},{10,12},{12,10},{14,8},{1,7},{3,5},... | collective-permute-start | bytes 589832 | tf_op jit(solution)/shard_map/ppermute | solution.py:385
  284.2 10.7 %copy-start.17 = (f32[48,8,128]{2,1,0:T(8,128)S(1)}, f32[48,8,128]{2,1,0:T(8,128)}, u32[]{:S(2)}) copy-start(f32[48,8,128]{2,1,0:T(8,128)} %get-tuple-element.104) | copy-start | bytes 589828
  294.8 8.4 %copy-start.9 = (f32[48,8,128]{2,1,0:T(8,128)}, f32[48,8,128]{2,1,0:T(8,128)S(1)}, u32[]{:S(2)}) copy-start(f32[48,8,128]{2,1,0:T(8,128)S(1)} %collective-permute-done.10.refs_1_) | copy-start | bytes 589828
  294.9 8.4 %collective-permute-start.21 = (f32[48,8,128]{2,1,0:T(8,128)S(1)}, f32[48,8,128]{2,1,0:T(8,128)S(1)}, u32[]{:S(2)}, u32[]{:S(2)}) collective-permute-start(f32[48,8,128]{2,1,0:T(8,128)S(1)} %copy-done.17), channel_id=1, source_target_pairs={{0,12},{2,14},{4,8},{6,10},{8,4},{10,6},{12,0},{14,2},{1,13},{3,15... | collective-permute-start | bytes 589832 | tf_op jit(solution)/shard_map/ppermute | solution.py:385
  298.2 5.0 %copy-start.10 = (f32[48,8,128]{2,1,0:T(8,128)}, f32[48,8,128]{2,1,0:T(8,128)S(1)}, u32[]{:S(2)}) copy-start(f32[48,8,128]{2,1,0:T(8,128)S(1)} %collective-permute-done.20.refs_5_) | copy-start | bytes 589828
  298.3 5.0 %copy-start.11 = (f32[48,8,128]{2,1,0:T(8,128)}, f32[48,8,128]{2,1,0:T(8,128)S(1)}, u32[]{:S(2)}) copy-start(f32[48,8,128]{2,1,0:T(8,128)S(1)} %collective-permute-done.12.refs_2_) | copy-start | bytes 589828
  298.3 5.0 %copy-start.12 = (f32[48,8,128]{2,1,0:T(8,128)}, f32[48,8,128]{2,1,0:T(8,128)S(1)}, u32[]{:S(2)}) copy-start(f32[48,8,128]{2,1,0:T(8,128)S(1)} %collective-permute-done.22.refs_7_) | copy-start | bytes 589828
  298.3 5.0 %copy-start.13 = (f32[48,8,128]{2,1,0:T(8,128)}, f32[48,8,128]{2,1,0:T(8,128)S(1)}, u32[]{:S(2)}) copy-start(f32[48,8,128]{2,1,0:T(8,128)S(1)} %collective-permute-done.15.refs_3_) | copy-start | bytes 589828
  303.3 0.7 copy-start.14
